TPU v7x, 256 devices: a whole 4x4x8 slice. The times are simulated.
256 devices in a mesh: req: 32 (over z, y), tp: 8 (over x, core).
Axes of the slice: x: 4, y: 4, z: 8, core: 2. Of those that a mesh axis runs over, the one named last changes fastest.
Arguments:
- hidden: bfloat16 [4096, 8192], P('req'), may hold values from -6 to 6
- input_norm_gain: bfloat16 [8192], replicated, may hold values from 0.25 to 1.75
- wq: bfloat16 [8192, 8192], P('req', 'tp'), as said below
- wk: bfloat16 [8192, 1024], P('req', 'tp'), as said below
- wv: bfloat16 [8192, 1024], P('req', 'tp'), may hold values from -0.0625 to 0.0625
- adapter_down_weight: bfloat16 [64, 48, 8192], P('req', None, 'tp'), may hold values from -0.0625 to 0.0625
- adapter_up_query: bfloat16 [64, 16, 8192], P('req', None, 'tp'), may hold values from -1.5 to 1.5
- adapter_up_key_value: bfloat16 [64, 32, 1024], P('req', None, 'tp'), may hold values from -1.5 to 1.5
- token_request_adapter: int32 [4096], P('req'), may hold values from 0 to 63, as said below
- adapter_storage_slot: int32 [64], replicated, may hold values from 0 to 63, as said below
Outputs:
- context: bfloat16 [4096, 8192], P('req', 'tp')
- keys: bfloat16 [4096, 1024], P('req', 'tp')
- values: bfloat16 [4096, 1024], P('req', 'tp')
Inputs may be any that keep to these rules, and one draw needn't show every extreme that they name: `token_request_adapter`: within each aligned block of 128 tokens (the tokens of one index of req), the tokens of one adapter form one contiguous prompt, different prompts of a block use adapters whose slots lie on different holders (slot // 2), and at most 8 tokens of a block use adapters of one holder; in every block some holder gets exactly 8. `adapter_storage_slot`: A permutation of the slots. `wq`: entries of order 8192^-0.5. `wk`: entries of order 8192^-0.5 or more.
All inputs are finite; a program needn't handle non-finite values.
Results may differ from a plain program's by a relative error of at most 0.012.
Values may be sent and summed in bfloat16 or wider, within the bound.
A program may use at most 128 MiB of HBM per device.

v0:
```python
import jax
import jax.numpy as jnp
from jax import lax
from jax.sharding import PartitionSpec as P

HEAD_SIZE = 128


def apply_up_projection(low_rank_product, selected_entries, table_q, table_kv, adapter_rank_value):
    held_adapters = selected_entries.shape[-1]

    def widen(piece):
        return (selected_entries[..., :, None] * piece[..., None, :]).reshape(
            piece.shape[:-1] + (held_adapters * adapter_rank_value,)
        )

    part_q = jnp.einsum(
        "...c,cw->...w",
        widen(low_rank_product[..., :adapter_rank_value]),
        table_q.reshape(held_adapters * adapter_rank_value, -1),
        preferred_element_type=jnp.float32,
    )
    part_k = jnp.einsum(
        "...c,cw->...w",
        widen(low_rank_product[..., adapter_rank_value : 2 * adapter_rank_value]),
        table_kv[:, :adapter_rank_value].reshape(held_adapters * adapter_rank_value, -1),
        preferred_element_type=jnp.float32,
    )
    part_v = jnp.einsum(
        "...c,cw->...w",
        widen(low_rank_product[..., 2 * adapter_rank_value :]),
        table_kv[:, adapter_rank_value:].reshape(held_adapters * adapter_rank_value, -1),
        preferred_element_type=jnp.float32,
    )
    return jnp.concatenate([part_q, part_k, part_v], axis=-1).astype(jnp.bfloat16)


def rotate(field, position, head_dim):
    count = field.shape[0]
    heads = field.shape[1] // head_dim
    half = head_dim // 2
    freq = 10000.0 ** (-(jnp.arange(half, dtype=jnp.float32) * 2.0 / head_dim))
    angle = position.astype(jnp.float32)[:, None] * freq[None, :]
    cosine = jnp.cos(angle)[:, None, :]
    sine = jnp.sin(angle)[:, None, :]
    shaped = field.reshape(count, heads, head_dim)
    first = shaped[..., :half]
    second = shaped[..., half:]
    turned = jnp.concatenate(
        [first * cosine - second * sine, second * cosine + first * sine], axis=-1
    )
    return turned.reshape(count, heads * head_dim)


def per_device(
    hidden,
    input_norm_gain,
    wq,
    wk,
    wv,
    adapter_down_weight,
    adapter_up_query,
    adapter_up_key_value,
    token_request_adapter,
    adapter_storage_slot,
):
    tokens = hidden.shape[0]
    n_req = lax.axis_size("req")
    held_adapters = adapter_down_weight.shape[0]
    rank_all_projections = adapter_down_weight.shape[1]
    adapter_rank_value = rank_all_projections // 3
    partition_width = adapter_down_weight.shape[2]
    q_width = wq.shape[1]
    key_value_width = wk.shape[1]
    head_dim = HEAD_SIZE
    wide = hidden.astype(jnp.float32)
    scale = lax.rsqrt(jnp.mean(wide * wide, axis=-1, keepdims=True) + 1e-05)
    normed = (wide * scale * input_norm_gain.astype(jnp.float32)[None, :]).astype(jnp.bfloat16)
    feature_part = lax.dynamic_slice_in_dim(
        normed, lax.axis_index("tp") * partition_width, partition_width, 1
    )
    count = adapter_storage_slot.shape[0]
    match = token_request_adapter[:, None] == jnp.arange(count, dtype=jnp.int32)[None, :]
    slot = jnp.sum(jnp.where(match, adapter_storage_slot[None, :], 0), axis=1)
    holder = slot // held_adapters
    within = slot % held_adapters
    steps = jnp.arange(tokens, dtype=jnp.int32)
    same = holder[:, None] == holder[None, :]
    earlier = same & (steps[None, :] < steps[:, None])
    position = jnp.sum(earlier.astype(jnp.int32), axis=1)
    visible = same & (steps[None, :] <= steps[:, None])
    pieces = (
        lax.all_gather(wq, "req", axis=0, tiled=True),
        lax.all_gather(wk, "req", axis=0, tiled=True),
        lax.all_gather(wv, "req", axis=0, tiled=True),
    )
    base_q, base_k, base_v = tuple(
        (jnp.dot(normed, piece, preferred_element_type=jnp.float32) for piece in pieces)
    )
    cap = 2 * tokens // n_req
    target = holder * cap + position
    placed = target[None, :] == jnp.arange(n_req * cap, dtype=jnp.int32)[:, None]
    place = placed.astype(jnp.bfloat16)
    send_rows = (
        jnp.dot(place, feature_part, preferred_element_type=jnp.float32)
        .astype(jnp.bfloat16)
        .reshape(n_req, cap, partition_width)
    )
    send_which = jnp.sum(jnp.where(placed, within[None, :], 0), axis=1).reshape(n_req, cap)
    rows = lax.all_to_all(send_rows, "req", split_axis=0, concat_axis=0, tiled=True)
    which = lax.all_to_all(send_which, "req", split_axis=0, concat_axis=0, tiled=True)
    adapter_table = adapter_down_weight.reshape(
        held_adapters * rank_all_projections, partition_width
    )
    partial_value = jnp.einsum(
        "skd,cd->skc", rows, adapter_table, preferred_element_type=jnp.float32
    )
    partial_value = partial_value.reshape(
        rows.shape[0], rows.shape[1], held_adapters, rank_all_projections
    )
    selected_entries = (which[..., None] == jnp.arange(held_adapters, dtype=jnp.int32)).astype(
        jnp.float32
    )
    low_part = jnp.sum(partial_value * selected_entries[..., None], axis=2)
    low_rank_product = lax.psum(low_part, "tp").astype(jnp.bfloat16)
    delta_row_values = apply_up_projection(
        low_rank_product,
        selected_entries.astype(jnp.bfloat16),
        adapter_up_query,
        adapter_up_key_value,
        adapter_rank_value,
    )
    returned = lax.all_to_all(delta_row_values, "req", split_axis=0, concat_axis=0, tiled=True)
    flat = returned.reshape(n_req * cap, returned.shape[-1])
    adapter_delta = lax.dot_general(
        place, flat, (((0,), (0,)), ((), ())), preferred_element_type=jnp.float32
    )
    query = base_q + 0.5 * adapter_delta[:, :q_width]
    key = base_k + 0.5 * adapter_delta[:, q_width : q_width + key_value_width]
    value = base_v + 0.5 * adapter_delta[:, q_width + key_value_width :]
    query_rotated = rotate(query, position, head_dim).astype(jnp.bfloat16)
    keys = rotate(key, position, head_dim).astype(jnp.bfloat16)
    values = value.astype(jnp.bfloat16)
    kv_heads = key_value_width // head_dim
    token_group = q_width // key_value_width
    block = min(tokens, 512)
    blocks = tokens // block
    query_block_list = query_rotated.reshape(blocks, block, kv_heads, token_group, head_dim)
    seen_blocks = visible.reshape(blocks, block, tokens)
    k_heads = keys.reshape(tokens, kv_heads, head_dim)
    v_heads = values.reshape(tokens, kv_heads, head_dim)

    def attend(items):
        q_here, seen = items
        scores = jnp.einsum(
            "tkgd,skd->kgts", q_here, k_heads, preferred_element_type=jnp.float32
        ) / jnp.sqrt(jnp.float32(head_dim))
        scores = jnp.where(seen[None, None, :, :], scores, jnp.float32(-1e30))
        top = jnp.max(scores, axis=-1, keepdims=True)
        raised = jnp.exp(scores - top)
        weights = (raised / jnp.sum(raised, axis=-1, keepdims=True)).astype(jnp.bfloat16)
        mixed = jnp.einsum("kgts,skd->tkgd", weights, v_heads, preferred_element_type=jnp.float32)
        return mixed.astype(jnp.bfloat16)

    context = lax.map(attend, (query_block_list, seen_blocks))
    return (context.reshape(tokens, q_width), keys, values)


def solution(mesh):
    in_specs = (
        P("req", None),
        P(),
        P("req", "tp"),
        P("req", "tp"),
        P("req", "tp"),
        P("req", None, "tp"),
        P("req", None, "tp"),
        P("req", None, "tp"),
        P("req"),
        P(),
    )
    out_specs = (P("req", "tp"), P("req", "tp"), P("req", "tp"))
    return jax.shard_map(
        per_device, mesh=mesh, in_specs=in_specs, out_specs=out_specs, check_vma=False
    )
```

profile of v0, /device:TPU:6, one launch (start us, length us, event | category | flops | bytes accessed | tf_op | source)
XLA Modules:
  0.0 328.9 jit_solution(802538345928479025)
XLA Ops:
  7.2 0.0 copy-start
  7.2 0.0 all-gather.6.cloned.1.call-start
  7.2 0.7 all-gather.6.cloned.1.call-update
  7.9 0.0 all-gather.4.cloned.1.call-start
  8.0 0.7 all-gather.4.cloned.1.call-update
  8.7 0.0 all-gather.8.cloned.1.call-start
  8.7 0.7 all-gather.8.cloned.1.call-update
  9.4 0.8 select_reduce_fusion.1
  10.2 0.1 convert_reduce_fusion
  10.3 0.1 select_reduce_fusion
  10.4 0.7 all_to_all.12
  11.1 11.5 %all-to-all-start = ((s32[32,1,8]{2,1,0:T(1,128)}), s32[32,1,8]{2,1,0:T(1,128)S(1)}, u32[]{:S(2)}, u32[]{:S(2)}) async-start(s32[32,1,8]{2,1,0:T(1,128)} %bitcast), calls=%async_computation | async-start | bytes 32768 | tf_op jit(solution)/shard_map/all_to_all | solution.py:111
  22.6 0.7 convert_element_type.72
  23.3 2.2 fusion
  25.6 0.6 fusion.2
  26.2 0.0 copy-start.4
  26.2 1.1 fusion.4
  27.3 5.0 %all-to-all-done = s32[32,1,8]{2,1,0:T(1,128)S(1)} async-done(((s32[32,1,8]{2,1,0:T(1,128)}), s32[32,1,8]{2,1,0:T(1,128)S(1)}, u32[]{:S(2)}, u32[]{:S(2)}) %all-to-all-start) | async-done | bytes 1056 | tf_op jit(solution)/shard_map/all_to_all | solution.py:111
  32.3 4.8 %all-to-all-start.1 = ((bf16[32,8,1024]{2,1,0:T(8,128)(2,1)}), bf16[32,8,1024]{2,1,0:T(8,128)(2,1)S(1)}, u32[]{:S(2)}, u32[]{:S(2)}) async-start(bf16[32,8,1024]{2,1,0:T(8,128)(2,1)} %fusion.4), calls=%async_computation.1 | async-start | bytes 1048576 | tf_op jit(solution)/shard_map/all_to_all | solution.py:110
  37.1 18.4 %all-to-all-done.1 = bf16[32,8,1024]{2,1,0:T(8,128)(2,1)S(1)} async-done(((bf16[32,8,1024]{2,1,0:T(8,128)(2,1)}), bf16[32,8,1024]{2,1,0:T(8,128)(2,1)S(1)}, u32[]{:S(2)}, u32[]{:S(2)}) %all-to-all-start.1) | async-done | bytes 524320 | tf_op jit(solution)/shard_map/all_to_all | solution.py:110
  55.5 0.3 fusion.8
  55.8 22.2 %psum.7 = bf16[32,8,48]{2,1,0:T(8,128)(2,1)S(1)} all-reduce(f32[32,8,48]{2,1,0:T(8,128)S(1)} %fusion.8), channel_id=1, replica_groups=mesh['req'=32,'tp'=8] {'tp'}, use_global_device_ids=true, to_apply=%region_5.6 | all-reduce | flops 12288 | bytes 73728 | tf_op jit(solution)/shard_map/psum | solution.py:125
  78.0 0.1 fusion.54
  78.1 0.3 fusion.9
  78.5 0.3 fusion.10
  78.8 0.2 copy-done.3
  79.0 0.4 fusion.3
  79.4 0.9 pad_maximum_fusion
  80.3 5.4 %all-to-all-start.2 = ((bf16[32,8,1280]{2,1,0:T(8,128)(2,1)}), bf16[32,8,1280]{2,1,0:T(8,128)(2,1)}, u32[]{:S(2)}, u32[]{:S(2)}) async-start(bf16[32,8,1280]{2,1,0:T(8,128)(2,1)} %pad_maximum_fusion), calls=%async_computation.2 | async-start | bytes 1310720 | tf_op jit(solution)/shard_map/all_to_all | solution.py:133
  85.7 0.1 compare_and_fusion
  85.8 0.3 multiply_cosine_fusion
  86.1 20.8 %all-to-all-done.2 = bf16[32,8,1280]{2,1,0:T(8,128)(2,1)} async-done(((bf16[32,8,1280]{2,1,0:T(8,128)(2,1)}), bf16[32,8,1280]{2,1,0:T(8,128)(2,1)}, u32[]{:S(2)}, u32[]{:S(2)}) %all-to-all-start.2) | async-done | bytes 655392 | tf_op jit(solution)/shard_map/all_to_all | solution.py:133
  106.9 1.4 fusion.13
  108.2 0.0 all-gather.6.cloned.1.call-done
  108.3 2.3 fusion.11
  110.6 0.3 fusion.31
  110.9 0.7 maximum_bitcast_fusion.2
  111.6 60.1 %all-gather.4.cloned.1.call-done = bf16[8192,128]{1,0:T(8,128)(2,1)} async-done(((bf16[256,128]{1,0:T(8,128)(2,1)}), bf16[8192,128]{1,0:T(8,128)(2,1)}) %all-gather.4.cloned.1.call-update) | async-done | bytes 2097168 | tf_op jit(solution)/shard_map/all_gather | solution.py:95
  171.7 2.3 fusion.12
  174.0 138.1 %all-gather.8.cloned.1.call-done = bf16[8192,1024]{1,0:T(8,128)(2,1)} async-done(((bf16[256,1024]{1,0:T(8,128)(2,1)}), bf16[8192,1024]{1,0:T(8,128)(2,1)}) %all-gather.8.cloned.1.call-update) | async-done | bytes 16777232 | tf_op jit(solution)/shard_map/all_gather | solution.py:93
  312.2 8.1 %fusion.6 = f32[16,8,8,128]{3,1,2,0:T(8,128)S(1)} fusion(bf16[128,8192]{1,0:T(8,128)(2,1)S(1)} %fusion.2, bf16[8192,1024]{1,0:T(8,128)(2,1)} %all-gather.8.cloned.1.call-done, f32[128,1280]{1,0:T(8,128)S(1)} %fusion.13), kind=kOutput, calls=%fused_computation.12 | convolution fusion | flops 2147745792 | bytes 19922944 | tf_op jit(solution)/shard_map/dot_general | solution.py:98
  320.3 0.1 copy.49
  320.4 0.2 fusion.53
  320.6 0.2 subtract_convert_fusion
  320.8 0.3 fusion.56
  321.1 0.1 fusion.16
  321.3 0.2 convolution_convert_fusion.1
  321.5 0.9 copy.38
  (12 shorter events, 0.1 us)
Async XLA Ops:
  7.2 48.3 %copy-start = (bf16[2,48,1024]{2,1,0:T(8,128)(2,1)S(1)}, bf16[2,48,1024]{2,1,0:T(8,128)(2,1)}, u32[]{:S(2)}) copy-start(bf16[2,48,1024]{2,1,0:T(8,128)(2,1)} %param.15) | copy-start | bytes 589828
  7.2 101.1 %all-gather.6.cloned.1.call-start = ((), (), s32[]{:S(2)}) async-start(), calls=%async_computation.4 | async-start | bytes 2162688 | tf_op jit(solution)/shard_map/all_gather | solution.py:94
  7.9 163.8 %all-gather.4.cloned.1.call-start = ((), (), s32[]{:S(2)}) async-start(), calls=%async_computation.3 | async-start | bytes 2162688 | tf_op jit(solution)/shard_map/all_gather | solution.py:95
  8.7 303.5 %all-gather.8.cloned.1.call-start = ((), (), s32[]{:S(2)}) async-start(), calls=%async_computation.5 | async-start | bytes 17301504 | tf_op jit(solution)/shard_map/all_gather | solution.py:93
  11.1 21.2 %all-to-all-start = ((s32[32,1,8]{2,1,0:T(1,128)}), s32[32,1,8]{2,1,0:T(1,128)S(1)}, u32[]{:S(2)}, u32[]{:S(2)}) async-start(s32[32,1,8]{2,1,0:T(1,128)} %bitcast), calls=%async_computation | async-start | bytes 32768 | tf_op jit(solution)/shard_map/all_to_all | solution.py:111
  23.3 2.2 copy-start.1
  26.2 51.9 %copy-start.4 = (bf16[2,32,128]{2,1,0:T(8,128)(2,1)S(1)}, bf16[2,32,128]{2,1,0:T(8,128)(2,1)}, u32[]{:S(2)}) copy-start(bf16[2,32,128]{2,1,0:T(8,128)(2,1)} %param.17) | copy-start | bytes 49156
  32.3 23.2 %all-to-all-start.1 = ((bf16[32,8,1024]{2,1,0:T(8,128)(2,1)}), bf16[32,8,1024]{2,1,0:T(8,128)(2,1)S(1)}, u32[]{:S(2)}, u32[]{:S(2)}) async-start(bf16[32,8,1024]{2,1,0:T(8,128)(2,1)} %fusion.4), calls=%async_computation.1 | async-start | bytes 1048576 | tf_op jit(solution)/shard_map/all_to_all | solution.py:110
  78.1 0.8 copy-start.3
  80.3 26.5 %all-to-all-start.2 = ((bf16[32,8,1280]{2,1,0:T(8,128)(2,1)}), bf16[32,8,1280]{2,1,0:T(8,128)(2,1)}, u32[]{:S(2)}, u32[]{:S(2)}) async-start(bf16[32,8,1280]{2,1,0:T(8,128)(2,1)} %pad_maximum_fusion), calls=%async_computation.2 | async-start | bytes 1310720 | tf_op jit(solution)/shard_map/all_to_all | solution.py:133
  174.0 147.2 %copy-start.2 = (bf16[128,128]{1,0:T(8,128)(2,1)}, bf16[128,128]{1,0:T(8,128)(2,1)S(1)}, u32[]{:S(2)}) copy-start(bf16[128,128]{1,0:T(8,128)(2,1)S(1)} %fusion.12) | copy-start | bytes 98308
Sparse Core Ops, SparseCore 0:
  10.6 83.6 all-gather.5
  96.9 74.7 all-gather.3
  174.3 137.8 all-gather.7
where the time goes:
time: 330 us; the launch traced here: 329 us
  waiting for transfers between devices  244 us (74%)
  blocking collectives  22.2 us (7%)
  starting transfers between devices  21.8 us (7%)
  matrix products  17.1 us (5%)
  between operations  14 us (4%)
  other arithmetic  7.18 us (2%)
    all_gather x1, waiting for transfers between devices, per_device(): lax.all_gather(wq, 'req', axis=0, tiled=True)  138 us
    all_gather x1, waiting for transfers between devices, per_device(): lax.all_gather(wv, 'req', axis=0, tiled=True)  60.1 us
    psum x1, blocking collectives, per_device(): low_rank_product = lax.psum(low_part, 'tp').astype(jnp.bfloat16)  22.2 us
    all_to_all x1, waiting for transfers between devices, per_device(): lax.all_to_all(delta_row_values, 'req', split_axis=0, concat_axis=0, tile...  20.8 us
    all_to_all x1, waiting for transfers between devices, per_device(): lax.all_to_all(send_rows, 'req', split_axis=0, concat_axis=0, tiled=True)  18.4 us
    dot_general x3, matrix products, per_device(): jnp.dot(normed, piece, preferred_element_type=jnp.float32)  12.7 us
    all_to_all x1, starting transfers between devices, per_device(): lax.all_to_all(send_which, 'req', split_axis=0, concat_axis=0, tiled=True)  11.5 us
  transfers between devices with their start and end apart: 6, of which 5 were waited for; matrix products, arithmetic and copies ran while one was open for 5% of the time, Pallas kernels for 0%

commit v1 on v0

v1 whole, which is shorter than its diff:
```python
import jax
import jax.numpy as jnp
from jax import lax
from jax.sharding import PartitionSpec as P

HEAD_SIZE = 128
NY = 4
NZ = 8
ROWS = 32


def rotate(field, position, head_dim):
    count = field.shape[0]
    heads = field.shape[1] // head_dim
    half = head_dim // 2
    freq = 10000.0 ** (-(jnp.arange(half, dtype=jnp.float32) * 2.0 / head_dim))
    angle = position.astype(jnp.float32)[:, None] * freq[None, :]
    cosine = jnp.cos(angle)[:, None, :]
    sine = jnp.sin(angle)[:, None, :]
    shaped = field.reshape(count, heads, head_dim)
    first = shaped[..., :half]
    second = shaped[..., half:]
    turned = jnp.concatenate(
        [first * cosine - second * sine, second * cosine + first * sine], axis=-1
    )
    return turned.reshape(count, heads * head_dim)


def per_device(
    hidden,
    input_norm_gain,
    wq,
    wk,
    wv,
    adapter_down_weight,
    adapter_up_query,
    adapter_up_key_value,
    token_request_adapter,
    adapter_storage_slot,
):
    groups_y = [[z * NY + y for y in range(NY)] for z in range(NZ)]
    groups_z = [[z * NY + y for z in range(NZ)] for y in range(NY)]
    tokens, width = hidden.shape
    my_req = lax.axis_index("req")
    my_z = my_req // NY
    my_tp = lax.axis_index("tp")
    part = width // NZ
    wide = hidden.astype(jnp.float32)
    scale = lax.rsqrt(jnp.mean(wide * wide, axis=-1, keepdims=True) + 1e-05)
    normed = (wide * scale * input_norm_gain.astype(jnp.float32)[None, :]).astype(jnp.bfloat16)

    count = adapter_storage_slot.shape[0]
    match = token_request_adapter[:, None] == jnp.arange(count, dtype=jnp.int32)[None, :]
    slot = jnp.sum(jnp.where(match, adapter_storage_slot[None, :], 0), axis=1)
    plane = slot // 8
    steps = jnp.arange(tokens, dtype=jnp.int32)
    before = steps[None, :] < steps[:, None]
    same = (slot[:, None] // 2) == (slot[None, :] // 2)
    position = jnp.sum((same & before).astype(jnp.int32), axis=1)
    visible = same & (steps[None, :] <= steps[:, None])
    rank = jnp.sum(((plane[:, None] == plane[None, :]) & before).astype(jnp.int32), axis=1)

    w_q = lax.all_gather(wq, "req", axis=0, tiled=True, axis_index_groups=groups_y)
    w_kv = lax.all_gather(
        jnp.concatenate([wk, wv], axis=1), "req", axis=0, tiled=True, axis_index_groups=groups_y
    )
    down = lax.all_gather(
        adapter_down_weight, "req", axis=0, tiled=True, axis_index_groups=groups_y
    )
    up_q = lax.all_gather(adapter_up_query, "req", axis=0, tiled=True, axis_index_groups=groups_y)
    up_kv = lax.all_gather(
        adapter_up_key_value, "req", axis=0, tiled=True, axis_index_groups=groups_y
    )

    mine = lax.dynamic_slice_in_dim(normed, my_tp * 16, 16, 0).reshape(16, NZ, part)
    got = lax.all_to_all(
        mine, "req", split_axis=1, concat_axis=1, axis_index_groups=groups_z, tiled=True
    )
    acts = lax.all_gather(got, "tp", axis=0, tiled=True)
    acts = jnp.swapaxes(acts, 0, 1).reshape(NZ * tokens, part)

    code = lax.all_gather(slot * 256 + rank, "req", axis=0, tiled=True, axis_index_groups=groups_z)
    all_slot = code // 256
    all_rank = code % 256

    target = plane * ROWS + rank
    place = (target[None, :] == jnp.arange(NZ * ROWS, dtype=jnp.int32)[:, None]).astype(
        jnp.bfloat16
    )
    feature_part = lax.dynamic_slice_in_dim(normed, my_tp * part, part, 1)
    rows = (
        jnp.dot(place, feature_part, preferred_element_type=jnp.float32)
        .astype(jnp.bfloat16)
        .reshape(NZ, ROWS, part)
    )
    rows = lax.all_to_all(
        rows, "req", split_axis=0, concat_axis=0, axis_index_groups=groups_z, tiled=True
    ).reshape(NZ * ROWS, part)
    low_all = lax.dot_general(
        rows, down.reshape(8 * 48, part), (((1,), (1,)), ((), ())),
        preferred_element_type=jnp.float32,
    )
    low_all = lax.psum(low_all, "tp")

    block = jnp.arange(NZ * tokens, dtype=jnp.int32) // tokens
    all_target = jnp.where(all_slot // 8 == my_z, block * ROWS + all_rank, -1)
    spread = (all_target[:, None] == jnp.arange(NZ * ROWS, dtype=jnp.int32)[None, :]).astype(
        jnp.bfloat16
    )
    low_tok = jnp.dot(
        spread, low_all.astype(jnp.bfloat16), preferred_element_type=jnp.float32
    ).reshape(NZ * tokens, 8, 48)
    pick = (all_slot % 8)[:, None] == jnp.arange(8, dtype=jnp.int32)[None, :]
    low_tok = jnp.where(pick[:, :, None], low_tok, 0.0).astype(jnp.bfloat16)

    def up(lo, table):
        return jnp.dot(
            low_tok[:, :, lo : lo + 16].reshape(NZ * tokens, 128),
            table.reshape(128, -1),
            preferred_element_type=jnp.float32,
        ).astype(jnp.bfloat16)

    delta = jnp.concatenate(
        [up(0, up_q), up(16, up_kv[:, :16]), up(32, up_kv[:, 16:])], axis=1
    ).astype(jnp.float32)
    base = jnp.concatenate(
        [
            jnp.dot(acts, w_q, preferred_element_type=jnp.float32),
            jnp.dot(acts, w_kv, preferred_element_type=jnp.float32),
        ],
        axis=1,
    )
    part_out = (base + 0.5 * delta).astype(jnp.bfloat16)
    full = lax.psum_scatter(
        part_out, "req", scatter_dimension=0, axis_index_groups=groups_z, tiled=True
    ).astype(jnp.float32)

    query = full[:, :1024]
    key = full[:, 1024:1152]
    value = full[:, 1152:]
    head_dim = HEAD_SIZE
    q_rot = rotate(query, position, head_dim).astype(jnp.bfloat16)
    keys = rotate(key, position, head_dim).astype(jnp.bfloat16)
    values = value.astype(jnp.bfloat16)
    q_heads = q_rot.reshape(tokens, 8, head_dim)
    scores = jnp.einsum(
        "tgd,sd->gts", q_heads, keys, preferred_element_type=jnp.float32
    ) / jnp.sqrt(jnp.float32(head_dim))
    scores = jnp.where(visible[None], scores, jnp.float32(-1e30))
    top = jnp.max(scores, axis=-1, keepdims=True)
    raised = jnp.exp(scores - top)
    weights = (raised / jnp.sum(raised, axis=-1, keepdims=True)).astype(jnp.bfloat16)
    context = jnp.einsum("gts,sd->tgd", weights, values, preferred_element_type=jnp.float32)
    return (context.astype(jnp.bfloat16).reshape(tokens, 1024), keys, values)


def solution(mesh):
    in_specs = (
        P("req", None),
        P(),
        P("req", "tp"),
        P("req", "tp"),
        P("req", "tp"),
        P("req", None, "tp"),
        P("req", None, "tp"),
        P("req", None, "tp"),
        P("req"),
        P(),
    )
    out_specs = (P("req", "tp"), P("req", "tp"), P("req", "tp"))
    return jax.shard_map(
        per_device, mesh=mesh, in_specs=in_specs, out_specs=out_specs, check_vma=False
    )
```

time: 330 us -> 205 us (0.62)
  waiting for transfers between devices: 244 us -> 42.9 us
  blocking collectives: 22.2 us -> 114 us
  starting transfers between devices: 21.8 us -> 3.61 us
  local copies, waits for them, and re-layouts: 2.17 us -> 11.6 us
  matrix products: 17.1 us -> 12.6 us
    all_gather x3 -> x2, waiting for transfers between devices: 198 us -> 0.01 us  [the longest x1 0.01 us: per_device(): acts = lax.all_gather(got, 'tp', axis=0, tiled=True)]
    all_gather x0 -> x5, blocking collectives: none -> 69.3 us  [the longest x1 16.3 us: per_device(): lax.all_gather(slot * 256 + rank, 'req', axis=0, tiled=True, axis_index_g...]
    all_to_all x3 -> x1, waiting for transfers between devices: 44.1 us -> 0.01 us  [per_device(): lax.all_to_all(rows, 'req', split_axis=0, concat_axis=0, axis_index_group...]
    unnamed x3 -> x4, waiting for transfers between devices: 2.06 us -> 42.9 us
    all_to_all x0 -> x1, blocking collectives: none -> 20.3 us  [per_device(): lax.all_to_all(mine, 'req', split_axis=1, concat_axis=1, axis_index_group...]
    all_to_all x3 -> x1, starting transfers between devices: 21.6 us -> 3.49 us  [per_device(): lax.all_to_all(rows, 'req', split_axis=0, concat_axis=0, axis_index_group...]
    unnamed x12 -> x29, local copies, waits for them, and re-layouts: 1.16 us -> 7.91 us
    dot_general x10 -> x9, matrix products: 16 us -> 10.2 us  [the longest x1 4.22 us: per_device(): jnp.dot(acts, w_q, preferred_element_type=jnp.float32)]
  transfers between devices with their start and end apart: 6 -> 4, of which waited for: 5 -> 1; matrix products, arithmetic and copies ran while one was open for 5% -> 5% of each run, Pallas kernels for 0% -> 0%
where the time goes in v1:
time: 205 us
  blocking collectives  114 us (56%)
  waiting for transfers between devices  42.9 us (21%)
  between operations  14.1 us (7%)
  matrix products  12.6 us (6%)
  local copies, waits for them, and re-layouts  11.6 us (6%)
  other arithmetic  6.11 us (3%)
  starting transfers between devices  3.61 us (2%)
    unnamed x4, waiting for transfers between devices  42.9 us
    psum x1, blocking collectives, per_device(): low_all = lax.psum(low_all, 'tp')  24.6 us
    all_to_all x1, blocking collectives, per_device(): lax.all_to_all(mine, 'req', split_axis=1, concat_axis=1, axis_index_group...  20.3 us
    all_gather x1, blocking collectives, per_device(): lax.all_gather(slot * 256 + rank, 'req', axis=0, tiled=True, axis_index_g...  16.3 us
    all_gather x1, blocking collectives, per_device(): lax.all_gather(jnp.concatenate([wk, wv], axis=1), 'req', axis=0, tiled=Tr...  13.9 us
    all_gather x1, blocking collectives, per_device(): lax.all_gather(adapter_up_query, 'req', axis=0, tiled=True, axis_index_gr...  13.7 us
    all_gather x1, blocking collectives, per_device(): lax.all_gather(adapter_down_weight, 'req', axis=0, tiled=True, axis_index...  13.3 us
    all_gather x1, blocking collectives, per_device(): lax.all_gather(adapter_up_key_value, 'req', axis=0, tiled=True, axis_inde...  12 us
  transfers between devices with their start and end apart: 4, of which 1 were waited for; matrix products, arithmetic and copies ran while one was open for 5% of the time, Pallas kernels for 0%

profile of v1, /device:TPU:6, one launch (start us, length us, event | category | flops | bytes accessed | tf_op | source)
XLA Modules:
  0.0 205.1 jit_solution(17895983667200554692)
XLA Ops:
  7.2 0.0 all-gather.4.cloned.1.call-start
  7.2 2.2 %fusion.2 = f32[128]{0:T(128)S(1)} fusion(bf16[128,8192]{1,0:T(8,128)(2,1)} %param.10), kind=kLoop, calls=%fused_computation.5 | loop fusion | flops 3145600 | bytes 2097664 | tf_op jit(solution)/shard_map/reduce_sum | solution.py:49
  9.5 0.7 convert_element_type.69
  10.2 0.6 fusion.4
  10.9 1.3 copy-done.3
  12.2 20.3 %all_to_all.10 = bf16[16,8,1024]{2,0,1:T(8,128)(2,1)S(1)} all-to-all(bf16[16,8,1024]{2,0,1:T(8,128)(2,1)S(1)} %bitcast.69), channel_id=1, replica_groups={{0,32,64,96,128,160,192,224},{8,40,72,104,136,168,200,232},{16,48,80,11..., dimensions={1} | all-to-all | bytes 524288 | tf_op jit(solution)/shard_map/all_to_all | solution.py:76
  32.5 0.9 copy.63
  33.4 0.0 all-gather.4.cloned.1.call-update
  33.4 0.1 select_reduce_fusion
  33.5 0.1 convert_reduce_fusion.1
  33.6 2.0 convolution_convert_fusion
  35.7 3.5 %all-to-all-start.1 = ((bf16[8,32,1024]{2,1,0:T(8,128)(2,1)}), bf16[8,32,1024]{2,1,0:T(8,128)(2,1)S(1)}, u32[]{:S(2)}, u32[]{:S(2)}) async-start(bf16[8,32,1024]{2,1,0:T(8,128)(2,1)} %bitcast.5), calls=%async_computation.1 | async-start | bytes 1048576 | tf_op jit(solution)/shard_map/all_to_all | solution.py:96
  39.2 0.0 all-gather.6.cloned.1.call-start
  39.2 0.7 all-gather.6.cloned.1.call-update
  39.9 0.0 reduce-scatter.4.cloned.1.call-start
  40.0 13.9 %all_gather.23 = bf16[1024,256]{1,0:T(8,128)(2,1)S(1)} all-gather(bf16[256,256]{1,0:T(8,128)(2,1)S(1)} %pad_maximum_fusion), channel_id=1, replica_groups={{0,8,16,24},{32,40,48,56},{64,72,80,88},{96,104,112,120},{128,136,144,1..., dimensions={0}, use_global_device_ids=true | all-gather | bytes 655360 | tf_op jit(solution)/shard_map/all_gather | solution.py:64
  54.0 16.3 %all-gather = s32[8,1,128]{2,1,0:T(1,128)S(1)} all-gather(s32[1,1,128]{2,1,0:T(1,128)S(1)} %get-tuple-element.37), channel_id=1, replica_groups={{0,32,64,96,128,160,192,224},{8,40,72,104,136,168,200,232},{16,48,80,11..., dimensions={0}, use_global_device_ids=true | all-gather | bytes 4608 | tf_op jit(solution)/shard_map/all_gather | solution.py:82
  70.3 12.0 %all_gather.27 = bf16[8,32,128]{2,1,0:T(8,128)(2,1)S(1)} all-gather(bf16[2,32,128]{2,1,0:T(8,128)(2,1)S(1)} %copy-done.8), channel_id=1, replica_groups={{0,8,16,24},{32,40,48,56},{64,72,80,88},{96,104,112,120},{128,136,144,1..., dimensions={0}, use_global_device_ids=true | all-gather | bytes 81920 | tf_op jit(solution)/shard_map/all_gather | solution.py:71
  82.3 13.7 %all_gather.26 = bf16[8,16,1024]{2,1,0:T(8,128)(2,1)S(1)} all-gather(bf16[2,16,1024]{2,1,0:T(8,128)(2,1)S(1)} %copy-done.5), channel_id=1, replica_groups={{0,8,16,24},{32,40,48,56},{64,72,80,88},{96,104,112,120},{128,136,144,1..., dimensions={0}, use_global_device_ids=true | all-gather | bytes 327680 | tf_op jit(solution)/shard_map/all_gather | solution.py:70
  96.1 13.3 %all_gather.25 = bf16[8,48,1024]{2,1,0:T(8,128)(2,1)S(1)} all-gather(bf16[2,48,1024]{2,1,0:T(8,128)(2,1)S(1)} %copy-done.4), channel_id=1, replica_groups={{0,8,16,24},{32,40,48,56},{64,72,80,88},{96,104,112,120},{128,136,144,1..., dimensions={0}, use_global_device_ids=true | all-gather | bytes 983040 | tf_op jit(solution)/shard_map/all_gather | solution.py:67
  109.4 0.5 fusion.67
  109.8 24.6 %all-reduce.1 = bf16[256,384]{1,0:T(8,128)(2,1)S(1)} all-reduce(f32[256,384]{1,0:T(8,128)S(1)} %fusion.67), channel_id=1, replica_groups=mesh['req'=32,'tp'=8] {'tp'}, use_global_device_ids=true, to_apply=%region_3.4 | all-reduce | flops 98304 | bytes 589824 | tf_op jit(solution)/shard_map/psum | solution.py:103
  134.4 0.6 fusion.11
  135.0 0.2 select_convert_fusion
  135.2 0.3 fusion.10
  135.4 0.3 fusion.9
  135.7 2.1 %bitcast_convert_fusion = bf16[1024,1024]{0,1:T(8,128)(2,1)} fusion(bf16[8,16,1024]{2,1,0:T(8,128)(2,1)S(1)} %all_gather.26, bf16[1024,8,48]{0,2,1:T(8,128)(2,1)S(1)} %select_convert_fusion), kind=kOutput, calls=%fused_computation.8 | convolution fusion | flops 269484032 | bytes 2621440 | tf_op jit(solution)/shard_map/dot_general | solution.py:117
  137.8 2.7 %copy.64 = bf16[128,8,1024]{2,0,1:T(8,128)(2,1)S(1)} copy(bf16[128,8,1024]{2,1,0:T(8,128)(2,1)} %all-gather.4.cloned.1.call-done) | data formatting | bytes 4194304 | tf_op jit(solution)/shard_map/all_gather | solution.py:79
  140.5 1.7 fusion.66
  142.3 4.2 %fusion.65 = f32[1024,1024]{0,1:T(8,128)S(1)} fusion(bf16[1024,1024]{1,0:T(8,128)(2,1)S(1)} %bitcast.63, bf16[1024,1024]{1,0:T(8,128)(2,1)} %all-gather.6.cloned.1.call-done), kind=kOutput, calls=%fused_computation.117 | convolution fusion | flops 2147483648 | bytes 8388608 | tf_op jit(solution)/shard_map/dot_general | solution.py:128
  146.5 1.1 fusion.1
  147.7 2.7 %copy.75 = bf16[1024,1280]{1,0:T(8,128)(2,1)} copy(bf16[1024,1280]{0,1:T(8,128)(2,1)S(1)} %fusion.1) | data formatting | bytes 5242880
  150.4 0.0 reduce-scatter.4.cloned.1.call-update
  150.4 0.1 convert_reduce_fusion
  150.5 0.1 compare_and_fusion.1
  150.6 0.3 multiply_cosine_fusion
  150.9 42.1 %reduce-scatter.4.cloned.1.call-done = bf16[128,1280]{1,0:T(8,128)(2,1)} async-done(((bf16[1024,1280]{1,0:T(8,128)(2,1)}), bf16[128,1280]{1,0:T(8,128)(2,1)}) %reduce-scatter.4.cloned.1.call-update) | async-done | bytes 327696
  193.0 1.2 copy.76
  194.4 0.2 copy.78
  194.6 0.2 copy.77
  194.8 0.2 fusion.30
  195.0 0.2 subtract_convert_fusion
  195.2 0.4 fusion.60
  195.6 0.3 fusion.8
  195.9 0.7 copy.71
  196.7 0.3 convolution_convert_fusion.1
  197.0 0.9 copy.69
  197.8 0.7 copy.70
  (40 shorter events, 0.3 us)
Async XLA Ops:
  7.2 3.0 %copy-start.1 = (bf16[128,8192]{1,0:T(8,128)(2,1)S(1)}, bf16[128,8192]{1,0:T(8,128)(2,1)}, u32[]{:S(2)}) copy-start(bf16[128,8192]{1,0:T(8,128)(2,1)} %param.10) | copy-start | bytes 6291460
  7.2 130.6 %all-gather.4.cloned.1.call-start = ((), (), s32[]{:S(2)}) async-start(), calls=%async_computation.3 | async-start | bytes 2359296 | tf_op jit(solution)/shard_map/all_gather | solution.py:79
  10.2 23.2 %copy-start.9 = (s32[64]{0:T(128)S(1)}, s32[64]{0:T(128)}, u32[]{:S(2)}) copy-start(s32[64]{0:T(128)} %param.19) | copy-start | bytes 772
  10.2 23.2 %copy-start.10 = (s32[128]{0:T(128)S(1)}, s32[128]{0:T(128)}, u32[]{:S(2)}) copy-start(s32[128]{0:T(128)} %param.18) | copy-start | bytes 1540
  10.8 1.3 copy-start.3
  12.2 27.8 %copy-start.6 = (bf16[256,128]{1,0:T(8,128)(2,1)S(1)}, bf16[256,128]{1,0:T(8,128)(2,1)}, u32[]{:S(2)}) copy-start(bf16[256,128]{1,0:T(8,128)(2,1)} %param.14) | copy-start | bytes 196612
  12.2 27.8 %copy-start.7 = (bf16[256,128]{1,0:T(8,128)(2,1)S(1)}, bf16[256,128]{1,0:T(8,128)(2,1)}, u32[]{:S(2)}) copy-start(bf16[256,128]{1,0:T(8,128)(2,1)} %param.13) | copy-start | bytes 196612
  12.2 58.1 %copy-start.8 = (bf16[2,32,128]{2,1,0:T(8,128)(2,1)S(1)}, bf16[2,32,128]{2,1,0:T(8,128)(2,1)}, u32[]{:S(2)}) copy-start(bf16[2,32,128]{2,1,0:T(8,128)(2,1)} %param.17) | copy-start | bytes 49156
  12.2 70.1 %copy-start.5 = (bf16[2,16,1024]{2,1,0:T(8,128)(2,1)S(1)}, bf16[2,16,1024]{2,1,0:T(8,128)(2,1)}, u32[]{:S(2)}) copy-start(bf16[2,16,1024]{2,1,0:T(8,128)(2,1)} %param.16) | copy-start | bytes 196612
  12.2 83.8 %copy-start.4 = (bf16[2,48,1024]{2,1,0:T(8,128)(2,1)S(1)}, bf16[2,48,1024]{2,1,0:T(8,128)(2,1)}, u32[]{:S(2)}) copy-start(bf16[2,48,1024]{2,1,0:T(8,128)(2,1)} %param.15) | copy-start | bytes 589828
  35.7 73.7 %all-to-all-start.1 = ((bf16[8,32,1024]{2,1,0:T(8,128)(2,1)}), bf16[8,32,1024]{2,1,0:T(8,128)(2,1)S(1)}, u32[]{:S(2)}, u32[]{:S(2)}) async-start(bf16[8,32,1024]{2,1,0:T(8,128)(2,1)} %bitcast.5), calls=%async_computation.1 | async-start | bytes 1048576 | tf_op jit(solution)/shard_map/all_to_all | solution.py:96
  39.2 103.1 %all-gather.6.cloned.1.call-start = ((), (), s32[]{:S(2)}) async-start(), calls=%async_computation.4 | async-start | bytes 2621440 | tf_op jit(solution)/shard_map/all_gather | solution.py:63
  39.9 153.1 %reduce-scatter.4.cloned.1.call-start = ((), (), s32[]{:S(2)}) async-start(), calls=%async_computation.5 | async-start | bytes 2949120
  142.3 4.2 %copy-start = (bf16[1024,1024]{0,1:T(8,128)(2,1)S(1)}, bf16[1024,1024]{0,1:T(8,128)(2,1)}, u32[]{:S(2)}) copy-start(bf16[1024,1024]{0,1:T(8,128)(2,1)} %bitcast_convert_fusion) | copy-start | bytes 6291460
  142.3 4.2 %copy-start.2 = (f32[1024,256]{0,1:T(8,128)S(1)}, f32[1024,256]{0,1:T(8,128)}, u32[]{:S(2)}) copy-start(f32[1024,256]{0,1:T(8,128)} %fusion.66) | copy-start | bytes 3145732
Sparse Core Ops, SparseCore 0:
  33.5 22.6 all-gather.3
  58.0 40.0 all-gather.5
  150.5 42.4 reduce-scatter.3

commit v2 on v1

v2 whole, which is shorter than its diff:
```python
import functools

import jax
import jax.numpy as jnp
import numpy as np
from jax import lax
from jax.experimental import pallas as pl
from jax.experimental.pallas import tpu as pltpu
from jax.sharding import PartitionSpec as P

MESH = pl.DeviceIdType.MESH
HEAD = 128
NY = 4
NZ = 8
NT = 8
TOK = 128
WIDTH = 8192
PART = 1024
CW = 256
ROWS = 32
CHUNKS = 5
BF = jnp.bfloat16
F32 = jnp.float32
ORDER = (0, 1, 7, 2, 6, 3, 5, 4)
POS = tuple(ORDER.index(r) for r in range(NZ))
GROUPS = ((1, 2), (3, 2), (5, 3))
AHEAD = 5


def longest(c, way):
    return 4 if way == (1 if c % 2 == 0 else 0) else 3


def body(
    hid, gain, tra, sas, rope, wq, wk, wv, dn, uq, ukv,
    ctx, kout, vout,
    hidv, scale, act, asend, meta_s, meta_r, rsend, rrecv,
    wqb, wkvb, db, uqb, ukvb,
    place, low_s, low_r, low_l, part, sendb, recvb, cosb, sinb, visb,
    loc_sem, y_ss, y_rs, a_ss, a_rs, m_ss, m_rs, r_ss, r_rs,
    x_ss, x_rs, p_ss, p_rs, l_ss, l_rs, z_ss, z_rs,
):
    req = lax.axis_index("req")
    tp = lax.axis_index("tp")
    z = req // NY
    y = req % NY
    core = tp % 2
    partner = tp + 1 - 2 * core

    def zdev(q):
        return {"req": lax.rem(z + q + NZ, NZ) * NY + y, "tp": tp}

    def ydev(q):
        return {"req": z * NY + lax.rem(y + q + NY, NY), "tp": tp}

    def tdev(q):
        return {"req": req, "tp": lax.rem(tp + q + NT, NT)}

    partner_dev = {"req": req, "tp": partner}

    def remote(src, dst, ss, rs, dev):
        return pltpu.make_async_remote_copy(
            src_ref=src, dst_ref=dst, send_sem=ss, recv_sem=rs, device_id=dev, device_id_type=MESH
        )

    pending = []

    def go(copy):
        copy.start()
        pending.append(copy)

    def rows2(buf, yb):
        return buf.at[pl.ds(2 * yb, 2)]

    def rows2h(buf, yb, h):
        return buf.at[pl.ds(2 * yb + h, 1)]

    def cols(buf, yb, lo, wide):
        return buf.at[pl.ds(pl.multiple_of(yb * 256, 256), 256), pl.ds(lo, wide)]

    def colsh(buf, yb, h, lo, wide):
        return buf.at[pl.ds(pl.multiple_of(yb * 256 + h * 128, 128), 128), pl.ds(lo, wide)]

    items = [
        (dn, functools.partial(rows2, db), functools.partial(rows2h, db)),
        (uq, functools.partial(rows2, uqb), functools.partial(rows2h, uqb)),
        (ukv, functools.partial(rows2, ukvb), functools.partial(rows2h, ukvb)),
        (wk, lambda b: cols(wkvb, b, 0, 128), lambda b, h: colsh(wkvb, b, h, 0, 128)),
        (wv, lambda b: cols(wkvb, b, 128, 128), lambda b, h: colsh(wkvb, b, h, 128, 128)),
    ]
    for j in range(4):
        items.append((
            wq.at[:, pl.ds(CW * j, CW)],
            lambda b, j=j: cols(wqb, b, CW * j, CW),
            lambda b, h, j=j: colsh(wqb, b, h, CW * j, CW),
        ))
    yl = lax.rem(y + NY - 1, NY)
    yr = lax.rem(y + 1, NY)

    def y_first(i, way):
        src, region, _ = items[i]
        return remote(
            src, region(y), y_ss.at[i, way], y_rs.at[i, way], ydev(1 if way == 0 else -1)
        )

    def y_second(i, way):
        _, _, half = items[i]
        ref = half(yl if way == 0 else yr, way)
        return remote(
            ref, ref, y_ss.at[i, 2 + way], y_rs.at[i, 2 + way], ydev(1 if way == 0 else -1)
        )

    def y_start(i):
        if i < len(items):
            go(y_first(i, 0))
            go(y_first(i, 1))

    def y_pump(i):
        for way in range(2):
            y_first(i, way).wait_recv()
            go(y_second(i, way))
        y_start(i + AHEAD)

    def y_wait(i):
        y_second(i, 0).wait_recv()
        y_second(i, 1).wait_recv()

    hid_copy = pltpu.make_async_copy(hid, hidv, loc_sem.at[0])
    hid_copy.start()
    own = []
    for i in range(len(items)):
        src, region, _ = items[i]
        copy = pltpu.make_async_copy(src, region(y), loc_sem.at[1 + i])
        copy.start()
        own.append(copy)

    barrier = pltpu.get_barrier_semaphore()
    for q in range(1, NZ):
        pl.semaphore_signal(barrier, inc=1, device_id=zdev(q), device_id_type=MESH)
    for q in range(1, NT):
        pl.semaphore_signal(barrier, inc=1, device_id=tdev(q), device_id_type=MESH)
    for q in (1, -1):
        pl.semaphore_signal(barrier, inc=1, device_id=ydev(q), device_id_type=MESH)

    lane = lax.broadcasted_iota(jnp.int32, (TOK, TOK), 1)
    sub = lax.broadcasted_iota(jnp.int32, (TOK, TOK), 0)
    tra_c = jnp.transpose(jnp.broadcast_to(tra[...].astype(F32), (TOK, TOK))).astype(jnp.int32)
    sas_r = jnp.broadcast_to(sas[...].astype(F32), (TOK, TOK))
    slot_c = jnp.sum(jnp.where(tra_c == lane, sas_r, 0.0), axis=1, keepdims=True)
    slot_cm = jnp.broadcast_to(slot_c, (TOK, TOK))
    slot_rm = jnp.transpose(slot_cm).astype(jnp.int32)
    slot_cm = slot_cm.astype(jnp.int32)
    same = (slot_cm >> 1) == (slot_rm >> 1)
    pos_c = jnp.sum(jnp.where(same & (lane < sub), 1.0, 0.0), axis=1, keepdims=True)
    visb[...] = jnp.where(same & (lane <= sub), 1.0, 0.0)
    flat = (slot_cm >> 3) == (slot_rm >> 3)
    rank_r = jnp.sum(jnp.where(flat & (sub < lane), 1.0, 0.0), axis=0, keepdims=True)
    slot_r = slot_rm[0:1, :]
    code_r = slot_r.astype(F32) * 32.0 + rank_r
    meta_s[...] = jnp.broadcast_to(code_r, (8, TOK))
    meta_r[:, 0:TOK] = jnp.broadcast_to(code_r, (8, TOK))
    pos_m = jnp.broadcast_to(pos_c, (TOK, TOK))
    cos = jnp.zeros((TOK, TOK), F32)
    sin = jnp.zeros((TOK, TOK), F32)
    for p in range(8):
        here = pos_m == float(p)
        cos = jnp.where(here, rope[p : p + 1, :], cos)
        sin = jnp.where(here, rope[8 + p : 9 + p, :], sin)
    cosb[...] = cos
    sinb[...] = sin

    hid_copy.wait()

    def stat(i, carry):
        rows = pl.ds(pl.multiple_of(i * 16, 16), 16)
        total = jnp.zeros((16, 128), F32)
        for k in range(8):
            x = hidv[rows, pl.ds(k * 1024, 1024)].astype(F32)
            x = x * x
            for m in range(8):
                total = total + x[:, 128 * m : 128 * m + 128]
        mean = jnp.sum(total, axis=1, keepdims=True) * (1.0 / WIDTH)
        scale[rows, :] = jnp.broadcast_to(lax.rsqrt(mean + 1e-05), (16, 128))
        return carry

    lax.fori_loop(0, 8, stat, 0)

    pl.semaphore_wait(barrier, 7 + 7 + 2)
    for i in range(AHEAD):
        y_start(i)

    my_rows = pl.ds(pl.multiple_of(tp * 16, 16), 16)
    s16 = scale[my_rows, :][:, 0:1]
    for j in range(NZ):
        c = pl.ds(j * PART, PART)
        asend[j] = (
            hidv[my_rows, c].astype(F32) * s16 * gain[0:1, c].astype(F32)
        ).astype(BF)

    def a_copy(q):
        k = POS[(-q) % NZ]
        return remote(
            asend.at[lax.rem(z + q, NZ)], act.at[k, my_rows, :],
            a_ss.at[k], a_rs.at[k], zdev(q),
        )

    def m_copy(q):
        k = POS[(-q) % NZ]
        return remote(
            meta_s, meta_r.at[:, pl.ds(k * TOK, TOK)], m_ss.at[k], m_rs.at[k], zdev(q)
        )

    for q in ORDER[1:]:
        go(a_copy(q))
    for q in ORDER[1:]:
        go(m_copy(q))

    def normed(start):
        c = pl.ds(pl.multiple_of(start, PART), PART)
        return (hidv[:, c].astype(F32) * scale[:, 0:1] * gain[0:1, c].astype(F32)).astype(BF)

    target = (slot_rm >> 3) * ROWS + jnp.broadcast_to(rank_r, (TOK, TOK)).astype(jnp.int32)
    sub2 = lax.broadcasted_iota(jnp.int32, (NZ * ROWS, TOK), 0)
    put = jnp.where(
        sub2 == jnp.concatenate([target, target], axis=0), 1.0, 0.0
    ).astype(BF)
    rsend[...] = jnp.dot(put, normed(tp * PART), preferred_element_type=F32).astype(BF)

    def r_block(b):
        return pl.ds(pl.multiple_of(b * ROWS, ROWS), ROWS)

    def r_copy(q):
        k = POS[(-q) % NZ]
        return remote(
            rsend.at[r_block(lax.rem(z + q, NZ)), :], rrecv.at[pl.ds(k * ROWS, ROWS), :],
            r_ss.at[k], r_rs.at[k], zdev(q),
        )

    for q in ORDER[1:]:
        go(r_copy(q))
    rrecv[0:ROWS, :] = rsend[r_block(z), :]
    act[0] = normed(z * PART)

    def t_rows(q):
        return pl.ds(pl.multiple_of(lax.rem(tp + q + NT, NT) * 16, 16), 16)

    def x_region(g, q, half=None):
        lo, n = GROUPS[g]
        if half is None:
            return act.at[pl.ds(lo, n), t_rows(q), :]
        return act.at[pl.ds(lo, n), t_rows(q), pl.ds(512 * half, 512)]

    def x_first(g, way):
        ref = x_region(g, 0)
        return remote(ref, ref, x_ss.at[g, way], x_rs.at[g, way], tdev(2 if way == 0 else -2))

    def x_second(g, way):
        ref = x_region(g, -2 if way == 0 else 2, way)
        return remote(
            ref, ref, x_ss.at[g, 2 + way], x_rs.at[g, 2 + way], tdev(2 if way == 0 else -2)
        )

    def p_copy(g, k):
        ref = x_region(g, (0, -2, 2, 4)[k])
        return remote(ref, ref, p_ss.at[g, k], p_rs.at[g, k], partner_dev)

    def x_send(g):
        lo, n = GROUPS[g]
        for k in range(lo, lo + n):
            a_copy((-ORDER[k]) % NZ).wait_recv()
        go(x_first(g, 0))
        go(x_first(g, 1))
        go(p_copy(g, 0))

    def x_forward(g):
        for way in range(2):
            x_first(g, way).wait_recv()
            go(x_second(g, way))
            go(p_copy(g, 1 + way))

    def x_last(g):
        x_second(g, 0).wait_recv()
        x_second(g, 1).wait_recv()
        go(p_copy(g, 3))

    x_send(0)
    x_send(1)
    y_pump(0)
    x_send(2)
    x_forward(0)
    y_pump(1)
    y_pump(2)
    x_forward(1)
    x_last(0)
    y_pump(3)
    x_forward(2)
    x_last(1)
    y_pump(4)
    x_last(2)
    for g in range(3):
        for k in range(4):
            p_copy(g, k).wait_recv()

    for copy in own:
        copy.wait()

    def base(c):
        def tile(i, carry):
            a = act[pl.ds(2 * i, 2)].reshape(2 * TOK, PART)
            w = wkvb[...] if c == 0 else wqb[:, CW * (c - 1) : CW * c]
            part[c, pl.ds(2 * i, 2)] = jnp.dot(a, w, preferred_element_type=F32).reshape(
                2, TOK, CW
            )
            return carry

        lax.fori_loop(0, NZ // 2, tile, 0)

    y_wait(3)
    y_wait(4)
    base(0)
    y_pump(5)

    for q in ORDER[1:]:
        m_copy(q).wait_recv()
    lane2 = lax.broadcasted_iota(jnp.int32, (TOK, NZ * ROWS), 1)
    a8_row = jnp.zeros((8, NZ * ROWS), F32)
    for k in range(NZ):
        code = meta_r[0:8, k * TOK : (k + 1) * TOK]
        code_c = jnp.transpose(jnp.broadcast_to(code[0:1, :], (TOK, TOK))).astype(jnp.int32)
        slot_k = code_c[:, 0:1] >> 5
        rank_k = code_c[:, 0:1] & 31
        want = jnp.where((slot_k >> 3) == z, k * ROWS + rank_k, -1)
        hot = jnp.where(lane2 == want, 1.0, 0.0).astype(BF)
        place[k] = hot
        a8 = ((code.astype(jnp.int32) >> 5) & 7).astype(F32).astype(BF)
        a8_row = a8_row + jnp.dot(a8, hot, preferred_element_type=F32)

    y_wait(0)
    for q in ORDER[1:]:
        r_copy(q).wait_recv()
    low_all = lax.dot_general(
        db[...].reshape(8 * 48, PART), rrecv[...], (((1,), (1,)), ((), ())),
        preferred_element_type=F32,
    )
    low_mine = jnp.zeros((48, NZ * ROWS), F32)
    for a in range(8):
        low_mine = low_mine + jnp.where(
            a8_row[0:1, :] == float(a), low_all[48 * a : 48 * a + 48, :], 0.0
        )
    low_s[...] = low_mine.astype(BF)

    def l_copy(q):
        return remote(low_s, low_r.at[q], l_ss.at[q], l_rs.at[q], tdev(q))

    for q in range(1, NT):
        go(l_copy(q))
    y_wait(5)
    base(1)
    y_pump(6)
    for q in range(1, NT):
        l_copy(q).wait_recv()
    low_sum = low_mine
    for q in range(1, NT):
        low_sum = low_sum + low_r[q].astype(F32)
    low_sum = low_sum.astype(BF)
    wide = jnp.concatenate(
        [low_sum[0:16]] * 8 + [low_sum[16:32]] * 8 + [low_sum[32:48]] * 8, axis=0
    )
    lane3 = lax.broadcasted_iota(jnp.int32, (TOK, 384), 1)
    for k in range(NZ):
        code = meta_r[0:1, k * TOK : (k + 1) * TOK]
        code_c = jnp.transpose(jnp.broadcast_to(code, (TOK, TOK))).astype(jnp.int32)
        a8_k = (code_c[:, 0:1] >> 5) & 7
        got = lax.dot_general(
            place[k], wide, (((1,), (1,)), ((), ())), preferred_element_type=F32
        )
        low_l[k] = jnp.where(((lane3 >> 4) & 7) == a8_k, got, 0.0).astype(BF)

    y_wait(1)
    y_wait(2)

    def z_copy(c, way, h):
        k = POS[h if way == 0 else NZ - h]
        return remote(
            sendb.at[c, k], recvb.at[c, way, h - 1], z_ss.at[c, way, h - 1],
            z_rs.at[c, way, h - 1], zdev(1 if way == 0 else -1),
        )

    def correct(c):
        def tile(i, carry):
            ll = low_l[pl.ds(2 * i, 2)].reshape(2 * TOK, 384)
            if c == 0:
                u_k = ukvb[:, 0:16, :].reshape(128, 128)
                u_v = ukvb[:, 16:32, :].reshape(128, 128)
                d = jnp.concatenate(
                    [
                        jnp.dot(ll[:, 128:256], u_k, preferred_element_type=F32),
                        jnp.dot(ll[:, 256:384], u_v, preferred_element_type=F32),
                    ],
                    axis=1,
                )
            else:
                u_q = uqb[:, :, CW * (c - 1) : CW * c].reshape(128, CW)
                d = jnp.dot(ll[:, 0:128], u_q, preferred_element_type=F32)
            d = 0.5 * d.astype(BF).astype(F32)
            part[c, pl.ds(2 * i, 2)] += d.reshape(2, TOK, CW)
            return carry

        lax.fori_loop(0, NZ // 2, tile, 0)

    for c in range(CHUNKS):
        if c >= 2:
            y_wait(4 + c)
            base(c)
            if c < 4:
                y_pump(5 + c)
        correct(c)
        way = 0 if longest(c, 0) == 4 else 1
        k = POS[4]
        sendb[c, k] = part[c, k].astype(BF)
        go(z_copy(c, way, 4))
    for h in (3, 2, 1):
        for c in range(CHUNKS):
            for way in range(2):
                k = POS[h if way == 0 else NZ - h]
                total = part[c, k]
                if h + 1 <= longest(c, way):
                    z_copy(c, way, h + 1).wait_recv()
                    total = total + recvb[c, way, h].astype(F32)
                sendb[c, k] = total.astype(BF)
                go(z_copy(c, way, h))

    def final(c):
        z_copy(c, 0, 1).wait_recv()
        z_copy(c, 1, 1).wait_recv()
        return part[c, 0] + recvb[c, 0, 0].astype(F32) + recvb[c, 1, 0].astype(F32)

    cos = cosb[...]
    sin = sinb[...]

    def turn(u):
        return u * cos + pltpu.roll(u, HEAD // 2, 1) * sin

    kv = final(0)
    keys = turn(kv[:, 0:HEAD]).astype(BF)
    values = kv[:, HEAD:].astype(BF)
    kout[...] = keys
    vout[...] = values
    seen = visb[...] > 0.5
    root = float(np.float32(1.0) / np.sqrt(np.float32(HEAD)))
    for c in range(1, CHUNKS):
        both = final(c)
        for i in range(2):
            query = turn(both[:, HEAD * i : HEAD * (i + 1)]).astype(BF)
            scores = lax.dot_general(
                query, keys, (((1,), (1,)), ((), ())), preferred_element_type=F32
            ) * root
            scores = jnp.where(seen, scores, -1e30)
            raised = jnp.exp(scores - jnp.max(scores, axis=1, keepdims=True))
            weights = (raised / jnp.sum(raised, axis=1, keepdims=True)).astype(BF)
            lo = CW * (c - 1) + HEAD * i
            ctx[:, lo : lo + HEAD] = jnp.dot(
                weights, values, preferred_element_type=F32
            ).astype(BF)

    for copy in pending:
        copy.wait_send()


def rope_table():
    half = HEAD // 2
    freq = np.float32(10000.0) ** (-(np.arange(half, dtype=np.float32) * np.float32(2.0) / HEAD))
    angle = np.arange(8, dtype=np.float32)[:, None] * freq[None, :].astype(np.float32)
    cos = np.cos(angle).astype(np.float32)
    sin = np.sin(angle).astype(np.float32)
    return np.concatenate(
        [np.concatenate([cos, cos], axis=1), np.concatenate([-sin, sin], axis=1)], axis=0
    )


def per_device(hidden, gain, wq, wk, wv, down, up_q, up_kv, adapter, storage):
    any_spec = pl.BlockSpec(memory_space=pl.ANY)
    vmem = pl.BlockSpec(memory_space=pltpu.VMEM)
    dma = pltpu.SemaphoreType.DMA
    count = storage.shape[0]
    call = pl.pallas_call(
        body,
        out_shape=(
            jax.ShapeDtypeStruct((TOK, PART), BF),
            jax.ShapeDtypeStruct((TOK, HEAD), BF),
            jax.ShapeDtypeStruct((TOK, HEAD), BF),
        ),
        in_specs=[any_spec, vmem, vmem, vmem, vmem] + [any_spec] * 6,
        out_specs=(vmem, vmem, vmem),
        scratch_shapes=[
            pltpu.VMEM((TOK, WIDTH), BF),
            pltpu.VMEM((TOK, 128), F32),
            pltpu.VMEM((NZ, TOK, PART), BF),
            pltpu.VMEM((NZ, 16, PART), BF),
            pltpu.VMEM((8, TOK), F32),
            pltpu.VMEM((8, NZ * TOK), F32),
            pltpu.VMEM((NZ * ROWS, PART), BF),
            pltpu.VMEM((NZ * ROWS, PART), BF),
            pltpu.VMEM((PART, PART), BF),
            pltpu.VMEM((PART, CW), BF),
            pltpu.VMEM((8, 48, PART), BF),
            pltpu.VMEM((8, 16, PART), BF),
            pltpu.VMEM((8, 32, HEAD), BF),
            pltpu.VMEM((NZ, TOK, NZ * ROWS), BF),
            pltpu.VMEM((48, NZ * ROWS), BF),
            pltpu.VMEM((NT, 48, NZ * ROWS), BF),
            pltpu.VMEM((NZ, TOK, 384), BF),
            pltpu.VMEM((CHUNKS, NZ, TOK, CW), F32),
            pltpu.VMEM((CHUNKS, NZ, TOK, CW), BF),
            pltpu.VMEM((CHUNKS, 2, 4, TOK, CW), BF),
            pltpu.VMEM((TOK, TOK), F32),
            pltpu.VMEM((TOK, TOK), F32),
            pltpu.VMEM((TOK, TOK), F32),
            dma((10,)),
            dma((9, 4)), dma((9, 4)),
            dma((NZ,)), dma((NZ,)),
            dma((NZ,)), dma((NZ,)),
            dma((NZ,)), dma((NZ,)),
            dma((3, 4)), dma((3, 4)),
            dma((3, 4)), dma((3, 4)),
            dma((NT,)), dma((NT,)),
            dma((CHUNKS, 2, 4)), dma((CHUNKS, 2, 4)),
        ],
        compiler_params=pltpu.CompilerParams(
            collective_id=0, has_side_effects=True, vmem_limit_bytes=60 * 1024 * 1024
        ),
    )
    return call(
        hidden,
        gain.reshape(1, WIDTH),
        adapter.reshape(1, TOK),
        jnp.pad(storage.reshape(1, count), ((0, 0), (0, TOK - count))),
        jnp.asarray(rope_table()),
        wq, wk, wv, down, up_q, up_kv,
    )


def solution(mesh):
    in_specs = (
        P("req", None),
        P(),
        P("req", "tp"),
        P("req", "tp"),
        P("req", "tp"),
        P("req", None, "tp"),
        P("req", None, "tp"),
        P("req", None, "tp"),
        P("req"),
        P(),
    )
    out_specs = (P("req", "tp"), P("req", "tp"), P("req", "tp"))
    return jax.shard_map(
        per_device, mesh=mesh, in_specs=in_specs, out_specs=out_specs, check_vma=False
    )
```

time: 205 us -> 92.3 us (0.45)
  blocking collectives: 114 us -> 0 us
  Pallas kernels: 0 us -> 83.4 us
  waiting for transfers between devices: 42.9 us -> 0 us
  between operations: 14.1 us -> 0.64 us
  matrix products: 12.6 us -> 0 us
  other arithmetic: 6.11 us -> 0 us
  local copies, waits for them, and re-layouts: 11.6 us -> 6.94 us
  starting transfers between devices: 3.61 us -> 0 us
    pallas_call x0 -> x1, Pallas kernels: none -> 83.4 us  [per_device(): call(hidden, gain.reshape(1, WIDTH), adapter.reshape(1, TOK), jnp.pad(sto...]
    all_gather x5 -> x0, blocking collectives: 69.3 us -> none  [the longest x1 16.3 us: per_device(): lax.all_gather(slot * 256 + rank, 'req', axis=0, tiled=True, axis_index_g...]
    unnamed x4 -> x0, waiting for transfers between devices: 42.9 us -> none
    psum x1 -> x0, blocking collectives: 24.6 us -> none  [per_device(): low_all = lax.psum(low_all, 'tp')]
    all_to_all x1 -> x0, blocking collectives: 20.3 us -> none  [per_device(): lax.all_to_all(mine, 'req', split_axis=1, concat_axis=1, axis_index_group...]
    dot_general x10 -> x0, matrix products: 12.2 us -> none  [the longest x1 4.22 us: per_device(): jnp.dot(acts, w_q, preferred_element_type=jnp.float32)]
    unnamed x29 -> x3, local copies, waits for them, and re-layouts: 7.91 us -> 4.42 us
    all_to_all x1 -> x0, starting transfers between devices: 3.49 us -> none  [per_device(): lax.all_to_all(rows, 'req', split_axis=0, concat_axis=0, axis_index_group...]
  transfers between devices with their start and end apart: 4 -> 0, of which waited for: 1 -> 0; matrix products, arithmetic and copies ran while one was open for 5% -> 0% of each run, Pallas kernels for 0% -> 0%
where the time goes in v2:
time: 92.3 us; the launch traced here: 90.9 us
  Pallas kernels  83.4 us (90%)
  local copies, waits for them, and re-layouts  6.94 us (8%)
    pallas_call x1, Pallas kernels, per_device(): call(hidden, gain.reshape(1, WIDTH), adapter.reshape(1, TOK), jnp.pad(sto...  83.4 us
    unnamed x3, local copies, waits for them, and re-layouts  4.42 us

profile of v2, /device:TPU:6, one launch (start us, length us, event | category | flops | bytes accessed | tf_op | source)
XLA Modules:
  0.0 90.9 jit_solution(1395543561561544772)
XLA Ops:
  0.6 1.2 %pad.4.sas = s32[1,128]{1,0:T(1,128)} pad(s32[1,64]{1,0:T(1,128)} %bitcast.3, s32[]{:T(128)} %constant.1.clone.1), padding=0_0x0_64 | pad | bytes 772 | tf_op jit(solution)/shard_map/jit(_pad)/pad | solution.py:537
  1.8 1.3 %reshape.15.gain = bf16[1,8192]{1,0:T(2,128)(2,1)} reshape(bf16[8192]{0:T(1024)(128)(2,1)} %param.12) | data formatting | bytes 32768 | tf_op jit(solution)/shard_map/reshape | solution.py:535
  3.2 83.4 %shard_map.130 = (bf16[128,1024]{1,0:T(8,128)(2,1)}, bf16[128,128]{1,0:T(8,128)(2,1)}, bf16[128,128]{1,0:T(8,128)(2,1)}) custom-call(bf16[128,8192]{1,0:T(8,128)(2,1)} %hid.1, bf16[1,8192]{1,0:T(2,128)(2,1)} %reshape.15.gain, s32[1,128]{1,0:T(1,128)} %bitcast.2, s32[1,128]{1,0:T(1,128)} %pad.4.sas, f32[16,128]{1,0:T(8,128)} %constant.4.clone.rope, ...), custom_call_target="tpu_custom_call" | custom-call | tf_op jit(solution)/shard_map/pallas_call | solution.py:533
  86.5 1.7 %copy.17 = bf16[128,1024]{1,0:T(8,128)(2,1)} copy(bf16[128,1024]{1,0:T(8,128)(2,1)} %get-tuple-element.6) | data formatting | bytes 524288
  88.2 1.4 %copy.18 = bf16[128,128]{1,0:T(8,128)(2,1)} copy(bf16[128,128]{1,0:T(8,128)(2,1)} %get-tuple-element.7) | data formatting | bytes 65536
  89.6 1.4 %copy.19 = bf16[128,128]{1,0:T(8,128)(2,1)} copy(bf16[128,128]{1,0:T(8,128)(2,1)} %get-tuple-element.8) | data formatting | bytes 65536

commit v3 on v2

--- a/solution.py
+++ b/solution.py
@@ -24,7 +24,7 @@
 ORDER = (0, 1, 7, 2, 6, 3, 5, 4)
 POS = tuple(ORDER.index(r) for r in range(NZ))
 GROUPS = ((1, 2), (3, 2), (5, 3))
-AHEAD = 5
+AHEAD = 3
 
 
 def longest(c, way):
@@ -34,9 +34,9 @@
 def body(
     hid, gain, tra, sas, rope, wq, wk, wv, dn, uq, ukv,
     ctx, kout, vout,
-    hidv, scale, act, asend, meta_s, meta_r, rsend, rrecv,
+    hidv, hid16, gainf, scale, act, asend, meta_s, meta_r, rsend, rrecv,
     wqb, wkvb, db, uqb, ukvb,
-    place, low_s, low_r, low_l, part, sendb, recvb, cosb, sinb, visb,
+    place, a8_of, low_s, low_r, low_l, part, sendb, recvb, cosb, sinb, visb,
     loc_sem, y_ss, y_rs, a_ss, a_rs, m_ss, m_rs, r_ss, r_rs,
     x_ss, x_rs, p_ss, p_rs, l_ss, l_rs, z_ss, z_rs,
 ):
@@ -125,15 +125,6 @@
         y_second(i, 0).wait_recv()
         y_second(i, 1).wait_recv()
 
-    hid_copy = pltpu.make_async_copy(hid, hidv, loc_sem.at[0])
-    hid_copy.start()
-    own = []
-    for i in range(len(items)):
-        src, region, _ = items[i]
-        copy = pltpu.make_async_copy(src, region(y), loc_sem.at[1 + i])
-        copy.start()
-        own.append(copy)
-
     barrier = pltpu.get_barrier_semaphore()
     for q in range(1, NZ):
         pl.semaphore_signal(barrier, inc=1, device_id=zdev(q), device_id_type=MESH)
@@ -141,12 +132,21 @@
         pl.semaphore_signal(barrier, inc=1, device_id=tdev(q), device_id_type=MESH)
     for q in (1, -1):
         pl.semaphore_signal(barrier, inc=1, device_id=ydev(q), device_id_type=MESH)
+    my_rows = pl.ds(pl.multiple_of(tp * 16, 16), 16)
+    few_copy = pltpu.make_async_copy(hid.at[my_rows, :], hid16, loc_sem.at[10])
+    few_copy.start()
+    hid_copy = pltpu.make_async_copy(hid, hidv, loc_sem.at[0])
+    hid_copy.start()
 
     lane = lax.broadcasted_iota(jnp.int32, (TOK, TOK), 1)
     sub = lax.broadcasted_iota(jnp.int32, (TOK, TOK), 0)
+    gainf[...] = gain[...].astype(F32)
     tra_c = jnp.transpose(jnp.broadcast_to(tra[...].astype(F32), (TOK, TOK))).astype(jnp.int32)
-    sas_r = jnp.broadcast_to(sas[...].astype(F32), (TOK, TOK))
-    slot_c = jnp.sum(jnp.where(tra_c == lane, sas_r, 0.0), axis=1, keepdims=True)
+    held = sas.shape[1]
+    sas_r = jnp.broadcast_to(sas[...].astype(F32), (TOK, held))
+    slot_c = jnp.sum(
+        jnp.where(tra_c[:, :held] == lane[:, :held], sas_r, 0.0), axis=1, keepdims=True
+    )
     slot_cm = jnp.broadcast_to(slot_c, (TOK, TOK))
     slot_rm = jnp.transpose(slot_cm).astype(jnp.int32)
     slot_cm = slot_cm.astype(jnp.int32)
@@ -169,32 +169,32 @@
     cosb[...] = cos
     sinb[...] = sin
 
-    hid_copy.wait()
-
-    def stat(i, carry):
-        rows = pl.ds(pl.multiple_of(i * 16, 16), 16)
+    pl.semaphore_wait(barrier, 7 + 7 + 2)
+    for i in range(AHEAD):
+        y_start(i)
+    own = []
+    for i in range(len(items)):
+        src, region, _ = items[i]
+        copy = pltpu.make_async_copy(src, region(y), loc_sem.at[1 + i])
+        copy.start()
+        own.append(copy)
+
+    def inverse_root(ref, rows):
         total = jnp.zeros((16, 128), F32)
         for k in range(8):
-            x = hidv[rows, pl.ds(k * 1024, 1024)].astype(F32)
+            x = ref[rows, pl.ds(k * 1024, 1024)].astype(F32)
             x = x * x
             for m in range(8):
                 total = total + x[:, 128 * m : 128 * m + 128]
-        mean = jnp.sum(total, axis=1, keepdims=True) * (1.0 / WIDTH)
-        scale[rows, :] = jnp.broadcast_to(lax.rsqrt(mean + 1e-05), (16, 128))
-        return carry
-
-    lax.fori_loop(0, 8, stat, 0)
-
-    pl.semaphore_wait(barrier, 7 + 7 + 2)
-    for i in range(AHEAD):
-        y_start(i)
-
-    my_rows = pl.ds(pl.multiple_of(tp * 16, 16), 16)
-    s16 = scale[my_rows, :][:, 0:1]
-    for j in range(NZ):
-        c = pl.ds(j * PART, PART)
-        asend[j] = (
-            hidv[my_rows, c].astype(F32) * s16 * gain[0:1, c].astype(F32)
+        return lax.rsqrt(jnp.sum(total, axis=1, keepdims=True) * (1.0 / WIDTH) + 1e-05)
+
+    few_copy.wait()
+    s16 = inverse_root(hid16, slice(None))
+    for m in range(WIDTH // 128):
+        c = slice(128 * m, 128 * m + 128)
+        d = 128 * (m % 8)
+        asend[m // 8, :, d : d + 128] = (
+            hid16[:, c].astype(F32) * s16 * gainf[m : m + 1, :]
         ).astype(BF)
 
     def a_copy(q):
@@ -215,16 +215,28 @@
     for q in ORDER[1:]:
         go(m_copy(q))
 
-    def normed(start):
-        c = pl.ds(pl.multiple_of(start, PART), PART)
-        return (hidv[:, c].astype(F32) * scale[:, 0:1] * gain[0:1, c].astype(F32)).astype(BF)
+    hid_copy.wait()
+
+    def stat(i, carry):
+        rows = pl.ds(pl.multiple_of(i * 16, 16), 16)
+        scale[rows, :] = jnp.broadcast_to(inverse_root(hidv, rows), (16, 128))
+        return carry
+
+    lax.fori_loop(0, 8, stat, 0)
+
+    def normed(b, m):
+        c = pl.ds(pl.multiple_of(b * PART + 128 * m, 128), 128)
+        g = gainf[pl.ds(pl.multiple_of(b * 8, 8), 8), :]
+        return (hidv[:, c].astype(F32) * scale[...] * g[m : m + 1, :]).astype(BF)
 
     target = (slot_rm >> 3) * ROWS + jnp.broadcast_to(rank_r, (TOK, TOK)).astype(jnp.int32)
     sub2 = lax.broadcasted_iota(jnp.int32, (NZ * ROWS, TOK), 0)
     put = jnp.where(
         sub2 == jnp.concatenate([target, target], axis=0), 1.0, 0.0
     ).astype(BF)
-    rsend[...] = jnp.dot(put, normed(tp * PART), preferred_element_type=F32).astype(BF)
+    for m in range(8):
+        act[0, :, 128 * m : 128 * m + 128] = normed(tp, m)
+    rsend[...] = jnp.dot(put, act[0], preferred_element_type=F32).astype(BF)
 
     def r_block(b):
         return pl.ds(pl.multiple_of(b * ROWS, ROWS), ROWS)
@@ -239,7 +251,8 @@
     for q in ORDER[1:]:
         go(r_copy(q))
     rrecv[0:ROWS, :] = rsend[r_block(z), :]
-    act[0] = normed(z * PART)
+    for m in range(8):
+        act[0, :, 128 * m : 128 * m + 128] = normed(z, m)
 
     def t_rows(q):
         return pl.ds(pl.multiple_of(lax.rem(tp + q + NT, NT) * 16, 16), 16)
@@ -287,11 +300,28 @@
     x_send(1)
     y_pump(0)
     x_send(2)
+    y_pump(1)
     x_forward(0)
-    y_pump(1)
     y_pump(2)
     x_forward(1)
     x_last(0)
+
+    for q in ORDER[1:]:
+        m_copy(q).wait_recv()
+    lane2 = lax.broadcasted_iota(jnp.int32, (TOK, NZ * ROWS), 1)
+    a8_row = jnp.zeros((8, NZ * ROWS), F32)
+    for k in range(NZ):
+        code = meta_r[0:8, k * TOK : (k + 1) * TOK]
+        code_m = jnp.transpose(jnp.broadcast_to(code[0:1, :], (TOK, TOK)))
+        code_c = code_m[:, 0:1].astype(jnp.int32)
+        slot_k = code_c >> 5
+        want = jnp.where((slot_k >> 3) == z, k * ROWS + (code_c & 31), -1)
+        hot = jnp.where(lane2 == want, 1.0, 0.0).astype(BF)
+        place[k] = hot
+        a8_of[k] = jnp.broadcast_to((slot_k & 7).astype(F32), (TOK, 128))
+        a8 = ((code.astype(jnp.int32) >> 5) & 7).astype(F32).astype(BF)
+        a8_row = a8_row + jnp.dot(a8, hot, preferred_element_type=F32)
+
     y_pump(3)
     x_forward(2)
     x_last(1)
@@ -304,13 +334,14 @@
     for copy in own:
         copy.wait()
 
+    def product(c, i):
+        a = act[pl.ds(2 * i, 2)].reshape(2 * TOK, PART)
+        w = wkvb[...] if c == 0 else wqb[:, CW * (c - 1) : CW * c]
+        return jnp.dot(a, w, preferred_element_type=F32).reshape(2, TOK, CW)
+
     def base(c):
         def tile(i, carry):
-            a = act[pl.ds(2 * i, 2)].reshape(2 * TOK, PART)
-            w = wkvb[...] if c == 0 else wqb[:, CW * (c - 1) : CW * c]
-            part[c, pl.ds(2 * i, 2)] = jnp.dot(a, w, preferred_element_type=F32).reshape(
-                2, TOK, CW
-            )
+            part[c, pl.ds(2 * i, 2)] = product(c, i)
             return carry
 
         lax.fori_loop(0, NZ // 2, tile, 0)
@@ -319,21 +350,6 @@
     y_wait(4)
     base(0)
     y_pump(5)
-
-    for q in ORDER[1:]:
-        m_copy(q).wait_recv()
-    lane2 = lax.broadcasted_iota(jnp.int32, (TOK, NZ * ROWS), 1)
-    a8_row = jnp.zeros((8, NZ * ROWS), F32)
-    for k in range(NZ):
-        code = meta_r[0:8, k * TOK : (k + 1) * TOK]
-        code_c = jnp.transpose(jnp.broadcast_to(code[0:1, :], (TOK, TOK))).astype(jnp.int32)
-        slot_k = code_c[:, 0:1] >> 5
-        rank_k = code_c[:, 0:1] & 31
-        want = jnp.where((slot_k >> 3) == z, k * ROWS + rank_k, -1)
-        hot = jnp.where(lane2 == want, 1.0, 0.0).astype(BF)
-        place[k] = hot
-        a8 = ((code.astype(jnp.int32) >> 5) & 7).astype(F32).astype(BF)
-        a8_row = a8_row + jnp.dot(a8, hot, preferred_element_type=F32)
 
     y_wait(0)
     for q in ORDER[1:]:
@@ -366,15 +382,12 @@
     wide = jnp.concatenate(
         [low_sum[0:16]] * 8 + [low_sum[16:32]] * 8 + [low_sum[32:48]] * 8, axis=0
     )
-    lane3 = lax.broadcasted_iota(jnp.int32, (TOK, 384), 1)
+    which = ((lax.broadcasted_iota(jnp.int32, (TOK, 384), 1) >> 4) & 7).astype(F32)
     for k in range(NZ):
-        code = meta_r[0:1, k * TOK : (k + 1) * TOK]
-        code_c = jnp.transpose(jnp.broadcast_to(code, (TOK, TOK))).astype(jnp.int32)
-        a8_k = (code_c[:, 0:1] >> 5) & 7
         got = lax.dot_general(
             place[k], wide, (((1,), (1,)), ((), ())), preferred_element_type=F32
         )
-        low_l[k] = jnp.where(((lane3 >> 4) & 7) == a8_k, got, 0.0).astype(BF)
+        low_l[k] = jnp.where(which == a8_of[k][:, 0:1], got, 0.0).astype(BF)
 
     y_wait(1)
     y_wait(2)
@@ -386,49 +399,60 @@
             z_rs.at[c, way, h - 1], zdev(1 if way == 0 else -1),
         )
 
-    def correct(c):
+    def change(c, i):
+        ll = low_l[pl.ds(2 * i, 2)].reshape(2 * TOK, 384)
+        if c == 0:
+            u_k = ukvb[:, 0:16, :].reshape(128, 128)
+            u_v = ukvb[:, 16:32, :].reshape(128, 128)
+            d = jnp.concatenate(
+                [
+                    jnp.dot(ll[:, 128:256], u_k, preferred_element_type=F32),
+                    jnp.dot(ll[:, 256:384], u_v, preferred_element_type=F32),
+                ],
+                axis=1,
+            )
+        else:
+            u_q = uqb[:, :, CW * (c - 1) : CW * c].reshape(128, CW)
+            d = jnp.dot(ll[:, 0:128], u_q, preferred_element_type=F32)
+        return (0.5 * d.astype(BF).astype(F32)).reshape(2, TOK, CW)
+
+    def complete(c):
         def tile(i, carry):
-            ll = low_l[pl.ds(2 * i, 2)].reshape(2 * TOK, 384)
-            if c == 0:
-                u_k = ukvb[:, 0:16, :].reshape(128, 128)
-                u_v = ukvb[:, 16:32, :].reshape(128, 128)
-                d = jnp.concatenate(
-                    [
-                        jnp.dot(ll[:, 128:256], u_k, preferred_element_type=F32),
-                        jnp.dot(ll[:, 256:384], u_v, preferred_element_type=F32),
-                    ],
-                    axis=1,
-                )
-            else:
-                u_q = uqb[:, :, CW * (c - 1) : CW * c].reshape(128, CW)
-                d = jnp.dot(ll[:, 0:128], u_q, preferred_element_type=F32)
-            d = 0.5 * d.astype(BF).astype(F32)
-            part[c, pl.ds(2 * i, 2)] += d.reshape(2, TOK, CW)
+            here = part[c, pl.ds(2 * i, 2)] if c < 2 else product(c, i)
+            part[c, pl.ds(2 * i, 2)] = here + change(c, i)
             return carry
 
         lax.fori_loop(0, NZ // 2, tile, 0)
 
-    for c in range(CHUNKS):
-        if c >= 2:
-            y_wait(4 + c)
-            base(c)
-            if c < 4:
-                y_pump(5 + c)
-        correct(c)
-        way = 0 if longest(c, 0) == 4 else 1
-        k = POS[4]
-        sendb[c, k] = part[c, k].astype(BF)
-        go(z_copy(c, way, 4))
-    for h in (3, 2, 1):
+    def ring(c, h):
+        for way in range(2):
+            if h > longest(c, way):
+                continue
+            k = POS[h if way == 0 else NZ - h]
+            total = part[c, k]
+            if h + 1 <= longest(c, way):
+                z_copy(c, way, h + 1).wait_recv()
+                total = total + recvb[c, way, h].astype(F32)
+            sendb[c, k] = total.astype(BF)
+            go(z_copy(c, way, h))
+
+    for c in range(2):
+        complete(c)
+        ring(c, 4)
+    y_pump(7)
+    ring(0, 3)
+    ring(1, 3)
+    for c in range(2, CHUNKS):
+        y_wait(4 + c)
+        complete(c)
+        ring(c, 4)
+        if c == 2:
+            y_pump(8)
+    for c in range(2, CHUNKS):
+        ring(c, 3)
+    for h in (2, 1):
         for c in range(CHUNKS):
-            for way in range(2):
-                k = POS[h if way == 0 else NZ - h]
-                total = part[c, k]
-                if h + 1 <= longest(c, way):
-                    z_copy(c, way, h + 1).wait_recv()
-                    total = total + recvb[c, way, h].astype(F32)
-                sendb[c, k] = total.astype(BF)
-                go(z_copy(c, way, h))
+            ring(c, h)
 
     def final(c):
         z_copy(c, 0, 1).wait_recv()
@@ -467,6 +491,12 @@
         copy.wait_send()
 
 
+def forward(a, b, c, ao, bo, co):
+    ao[...] = a[...]
+    bo[...] = b[...]
+    co[...] = c[...]
+
+
 def rope_table():
     half = HEAD // 2
     freq = np.float32(10000.0) ** (-(np.arange(half, dtype=np.float32) * np.float32(2.0) / HEAD))
@@ -494,6 +524,8 @@
         out_specs=(vmem, vmem, vmem),
         scratch_shapes=[
             pltpu.VMEM((TOK, WIDTH), BF),
+            pltpu.VMEM((16, WIDTH), BF),
+            pltpu.VMEM((WIDTH // 128, 128), F32),
             pltpu.VMEM((TOK, 128), F32),
             pltpu.VMEM((NZ, TOK, PART), BF),
             pltpu.VMEM((NZ, 16, PART), BF),
@@ -507,6 +539,7 @@
             pltpu.VMEM((8, 16, PART), BF),
             pltpu.VMEM((8, 32, HEAD), BF),
             pltpu.VMEM((NZ, TOK, NZ * ROWS), BF),
+            pltpu.VMEM((NZ, TOK, 128), F32),
             pltpu.VMEM((48, NZ * ROWS), BF),
             pltpu.VMEM((NT, 48, NZ * ROWS), BF),
             pltpu.VMEM((NZ, TOK, 384), BF),
@@ -516,7 +549,7 @@
             pltpu.VMEM((TOK, TOK), F32),
             pltpu.VMEM((TOK, TOK), F32),
             pltpu.VMEM((TOK, TOK), F32),
-            dma((10,)),
+            dma((11,)),
             dma((9, 4)), dma((9, 4)),
             dma((NZ,)), dma((NZ,)),
             dma((NZ,)), dma((NZ,)),
@@ -530,14 +563,20 @@
             collective_id=0, has_side_effects=True, vmem_limit_bytes=60 * 1024 * 1024
         ),
     )
-    return call(
+    outs = call(
         hidden,
-        gain.reshape(1, WIDTH),
+        gain.reshape(WIDTH // 128, 128),
         adapter.reshape(1, TOK),
-        jnp.pad(storage.reshape(1, count), ((0, 0), (0, TOK - count))),
+        storage.reshape(1, count),
         jnp.asarray(rope_table()),
         wq, wk, wv, down, up_q, up_kv,
     )
+    return pl.pallas_call(
+        forward,
+        out_shape=tuple(jax.ShapeDtypeStruct(o.shape, o.dtype) for o in outs),
+        in_specs=[vmem] * 3,
+        out_specs=(vmem,) * 3,
+    )(*outs)
 
 
 def solution(mesh):

time: 92.3 us -> 77.3 us (0.84); the launches traced: 90.9 us -> 77.2 us
  local copies, waits for them, and re-layouts: 6.94 us -> 0 us
  Pallas kernels: 83.4 us -> 76.5 us
    pallas_call x1 -> x2, Pallas kernels: 83.4 us -> 76.5 us  [the longest x1 74.8 us: per_device(): call(hidden, gain.reshape(WIDTH // 128, 128), adapter.reshape(1, TOK), st...]
    unnamed x3 -> x0, local copies, waits for them, and re-layouts: 4.42 us -> none
    reshape x1 -> x0, local copies, waits for them, and re-layouts: 1.35 us -> none  [per_device(): gain.reshape(1, WIDTH)]
    pad x1 -> x0, local copies, waits for them, and re-layouts: 1.17 us -> none  [per_device(): jnp.pad(storage.reshape(1, count), ((0, 0), (0, TOK - count)))]
where the time goes in v3:
time: 77.3 us; the launch traced here: 77.2 us
  Pallas kernels  76.5 us (99%)
    pallas_call x1, Pallas kernels, per_device(): call(hidden, gain.reshape(WIDTH // 128, 128), adapter.reshape(1, TOK), st...  74.8 us
    pallas_call x1, Pallas kernels, per_device(): pl.pallas_call(forward, out_shape=tuple((jax.ShapeDtypeStruct(o.shape, o....  1.7 us

profile of v3, /device:TPU:6, one launch (start us, length us, event | category | flops | bytes accessed | tf_op | source)
XLA Modules:
  0.0 77.2 jit_solution(14150893313207335717)
XLA Ops:
  0.6 74.8 %shard_map.130 = (bf16[128,1024]{1,0:T(8,128)(2,1)}, bf16[128,128]{1,0:T(8,128)(2,1)}, bf16[128,128]{1,0:T(8,128)(2,1)}) custom-call(bf16[128,8192]{1,0:T(8,128)(2,1)} %hid.1, bf16[64,128]{1,0:T(8,128)(2,1)} %bitcast.3, s32[1,128]{1,0:T(1,128)} %bitcast.4, s32[1,64]{1,0:T(1,128)} %bitcast.5, f32[16,128]{1,0:T(8,128)} %constant.2.clone.rope, ...), custom_call_target="tpu_custom_call" | custom-call | tf_op jit(solution)/shard_map/pallas_call | solution.py:566
  75.5 1.7 %shard_map.131 = (bf16[128,1024]{1,0:T(8,128)(2,1)}, bf16[128,128]{1,0:T(8,128)(2,1)}, bf16[128,128]{1,0:T(8,128)(2,1)}) custom-call(bf16[128,1024]{1,0:T(8,128)(2,1)} %get-tuple-element.6.a, bf16[128,128]{1,0:T(8,128)(2,1)} %get-tuple-element.7.b, bf16[128,128]{1,0:T(8,128)(2,1)} %get-tuple-element.8.c), custom_call_target="tpu_custom_call" | custom-call | tf_op jit(solution)/shard_map/pallas_call | solution.py:574

commit v4 on v3

--- a/solution.py
+++ b/solution.py
@@ -24,6 +24,7 @@
 ORDER = (0, 1, 7, 2, 6, 3, 5, 4)
 POS = tuple(ORDER.index(r) for r in range(NZ))
 GROUPS = ((1, 2), (3, 2), (5, 3))
+FAR_FIRST = (7, 6, 5, 4, 3, 2, 1)
 AHEAD = 3
 
 
@@ -32,9 +33,9 @@
 
 
 def body(
-    hid, gain, tra, sas, rope, wq, wk, wv, dn, uq, ukv,
+    hid, gain_h, tra_h, sas_h, rope_h, wq, wk, wv, dn, uq, ukv,
     ctx, kout, vout,
-    hidv, hid16, gainf, scale, act, asend, meta_s, meta_r, rsend, rrecv,
+    gain, tra, sas, rope, hidv, hid16, gainf, scale, act, asend, meta_s, meta_r, rsend, rrecv,
     wqb, wkvb, db, uqb, ukvb,
     place, a8_of, low_s, low_r, low_l, part, sendb, recvb, cosb, sinb, visb,
     loc_sem, y_ss, y_rs, a_ss, a_rs, m_ss, m_rs, r_ss, r_rs,
@@ -83,10 +84,10 @@
 
     items = [
         (dn, functools.partial(rows2, db), functools.partial(rows2h, db)),
+        (wk, lambda b: cols(wkvb, b, 0, 128), lambda b, h: colsh(wkvb, b, h, 0, 128)),
+        (wv, lambda b: cols(wkvb, b, 128, 128), lambda b, h: colsh(wkvb, b, h, 128, 128)),
         (uq, functools.partial(rows2, uqb), functools.partial(rows2h, uqb)),
         (ukv, functools.partial(rows2, ukvb), functools.partial(rows2h, ukvb)),
-        (wk, lambda b: cols(wkvb, b, 0, 128), lambda b, h: colsh(wkvb, b, h, 0, 128)),
-        (wv, lambda b: cols(wkvb, b, 128, 128), lambda b, h: colsh(wkvb, b, h, 128, 128)),
     ]
     for j in range(4):
         items.append((
@@ -135,12 +136,63 @@
     my_rows = pl.ds(pl.multiple_of(tp * 16, 16), 16)
     few_copy = pltpu.make_async_copy(hid.at[my_rows, :], hid16, loc_sem.at[10])
     few_copy.start()
+    small = []
+    for i, (src, dst) in enumerate(((gain_h, gain), (tra_h, tra), (sas_h, sas), (rope_h, rope))):
+        copy = pltpu.make_async_copy(src, dst, loc_sem.at[11 + i])
+        copy.start()
+        small.append(copy)
     hid_copy = pltpu.make_async_copy(hid, hidv, loc_sem.at[0])
     hid_copy.start()
 
+    pl.semaphore_wait(barrier, 7 + 7 + 2)
+    for i in range(AHEAD):
+        y_start(i)
+    own = []
+    for i in range(len(items)):
+        src, region, _ = items[i]
+        copy = pltpu.make_async_copy(src, region(y), loc_sem.at[1 + i])
+        copy.start()
+        own.append(copy)
+
+    def inverse_root(ref, rows):
+        total = jnp.zeros((16, 128), F32)
+        for k in range(8):
+            x = ref[rows, pl.ds(k * 1024, 1024)].astype(F32)
+            x = x * x
+            for m in range(8):
+                total = total + x[:, 128 * m : 128 * m + 128]
+        return lax.rsqrt(jnp.sum(total, axis=1, keepdims=True) * (1.0 / WIDTH) + 1e-05)
+
+    few_copy.wait()
+    for copy in small:
+        copy.wait()
+    gainf[...] = gain[...].astype(F32)
+    s16 = inverse_root(hid16, slice(None))
+    for m in range(WIDTH // 128):
+        c = slice(128 * m, 128 * m + 128)
+        d = 128 * (m % 8)
+        asend[m // 8, :, d : d + 128] = (
+            hid16[:, c].astype(F32) * s16 * gainf[m : m + 1, :]
+        ).astype(BF)
+
+    def a_copy(q):
+        k = POS[(-q) % NZ]
+        return remote(
+            asend.at[lax.rem(z + q, NZ)], act.at[k, my_rows, :],
+            a_ss.at[k], a_rs.at[k], zdev(q),
+        )
+
+    def m_copy(q):
+        k = POS[(-q) % NZ]
+        return remote(
+            meta_s, meta_r.at[:, pl.ds(k * TOK, TOK)], m_ss.at[k], m_rs.at[k], zdev(q)
+        )
+
+    for k in FAR_FIRST:
+        go(a_copy((-ORDER[k]) % NZ))
+
     lane = lax.broadcasted_iota(jnp.int32, (TOK, TOK), 1)
     sub = lax.broadcasted_iota(jnp.int32, (TOK, TOK), 0)
-    gainf[...] = gain[...].astype(F32)
     tra_c = jnp.transpose(jnp.broadcast_to(tra[...].astype(F32), (TOK, TOK))).astype(jnp.int32)
     held = sas.shape[1]
     sas_r = jnp.broadcast_to(sas[...].astype(F32), (TOK, held))
@@ -159,62 +211,8 @@
     code_r = slot_r.astype(F32) * 32.0 + rank_r
     meta_s[...] = jnp.broadcast_to(code_r, (8, TOK))
     meta_r[:, 0:TOK] = jnp.broadcast_to(code_r, (8, TOK))
-    pos_m = jnp.broadcast_to(pos_c, (TOK, TOK))
-    cos = jnp.zeros((TOK, TOK), F32)
-    sin = jnp.zeros((TOK, TOK), F32)
-    for p in range(8):
-        here = pos_m == float(p)
-        cos = jnp.where(here, rope[p : p + 1, :], cos)
-        sin = jnp.where(here, rope[8 + p : 9 + p, :], sin)
-    cosb[...] = cos
-    sinb[...] = sin
-
-    pl.semaphore_wait(barrier, 7 + 7 + 2)
-    for i in range(AHEAD):
-        y_start(i)
-    own = []
-    for i in range(len(items)):
-        src, region, _ = items[i]
-        copy = pltpu.make_async_copy(src, region(y), loc_sem.at[1 + i])
-        copy.start()
-        own.append(copy)
-
-    def inverse_root(ref, rows):
-        total = jnp.zeros((16, 128), F32)
-        for k in range(8):
-            x = ref[rows, pl.ds(k * 1024, 1024)].astype(F32)
-            x = x * x
-            for m in range(8):
-                total = total + x[:, 128 * m : 128 * m + 128]
-        return lax.rsqrt(jnp.sum(total, axis=1, keepdims=True) * (1.0 / WIDTH) + 1e-05)
-
-    few_copy.wait()
-    s16 = inverse_root(hid16, slice(None))
-    for m in range(WIDTH // 128):
-        c = slice(128 * m, 128 * m + 128)
-        d = 128 * (m % 8)
-        asend[m // 8, :, d : d + 128] = (
-            hid16[:, c].astype(F32) * s16 * gainf[m : m + 1, :]
-        ).astype(BF)
-
-    def a_copy(q):
-        k = POS[(-q) % NZ]
-        return remote(
-            asend.at[lax.rem(z + q, NZ)], act.at[k, my_rows, :],
-            a_ss.at[k], a_rs.at[k], zdev(q),
-        )
-
-    def m_copy(q):
-        k = POS[(-q) % NZ]
-        return remote(
-            meta_s, meta_r.at[:, pl.ds(k * TOK, TOK)], m_ss.at[k], m_rs.at[k], zdev(q)
-        )
-
-    for q in ORDER[1:]:
-        go(a_copy(q))
-    for q in ORDER[1:]:
-        go(m_copy(q))
-
+    for k in FAR_FIRST:
+        go(m_copy((-ORDER[k]) % NZ))
     hid_copy.wait()
 
     def stat(i, carry):
@@ -248,8 +246,8 @@
             r_ss.at[k], r_rs.at[k], zdev(q),
         )
 
-    for q in ORDER[1:]:
-        go(r_copy(q))
+    for k in FAR_FIRST:
+        go(r_copy((-ORDER[k]) % NZ))
     rrecv[0:ROWS, :] = rsend[r_block(z), :]
     for m in range(8):
         act[0, :, 128 * m : 128 * m + 128] = normed(z, m)
@@ -296,101 +294,103 @@
         x_second(g, 1).wait_recv()
         go(p_copy(g, 3))
 
+    x_send(2)
+    y_pump(0)
+    x_send(1)
+    y_pump(1)
     x_send(0)
-    x_send(1)
-    y_pump(0)
-    x_send(2)
-    y_pump(1)
-    x_forward(0)
+    x_forward(2)
     y_pump(2)
     x_forward(1)
-    x_last(0)
+    x_last(2)
 
     for q in ORDER[1:]:
         m_copy(q).wait_recv()
-    lane2 = lax.broadcasted_iota(jnp.int32, (TOK, NZ * ROWS), 1)
-    a8_row = jnp.zeros((8, NZ * ROWS), F32)
+    a8_row = [jnp.zeros((8, TOK), F32) for _ in range(2)]
     for k in range(NZ):
         code = meta_r[0:8, k * TOK : (k + 1) * TOK]
-        code_m = jnp.transpose(jnp.broadcast_to(code[0:1, :], (TOK, TOK)))
-        code_c = code_m[:, 0:1].astype(jnp.int32)
-        slot_k = code_c >> 5
-        want = jnp.where((slot_k >> 3) == z, k * ROWS + (code_c & 31), -1)
-        hot = jnp.where(lane2 == want, 1.0, 0.0).astype(BF)
+        code_m = jnp.transpose(jnp.broadcast_to(code[0:1, :], (TOK, TOK))).astype(jnp.int32)
+        slot_k = code_m >> 5
+        want = jnp.where((slot_k >> 3) == z, (k % 4) * ROWS + (code_m & 31), -1)
+        hot = jnp.where(lane == want, 1.0, 0.0).astype(BF)
         place[k] = hot
-        a8_of[k] = jnp.broadcast_to((slot_k & 7).astype(F32), (TOK, 128))
+        a8_of[k] = (slot_k & 7).astype(F32)
         a8 = ((code.astype(jnp.int32) >> 5) & 7).astype(F32).astype(BF)
-        a8_row = a8_row + jnp.dot(a8, hot, preferred_element_type=F32)
+        a8_row[k // 4] = a8_row[k // 4] + jnp.dot(a8, hot, preferred_element_type=F32)
 
     y_pump(3)
-    x_forward(2)
+    x_forward(0)
     x_last(1)
     y_pump(4)
-    x_last(2)
-    for g in range(3):
-        for k in range(4):
-            p_copy(g, k).wait_recv()
-
-    for copy in own:
-        copy.wait()
+    x_last(0)
+
+    low_mine = [None, None]
+
+    def l_copy(g, q):
+        return remote(low_s.at[g], low_r.at[g, q], l_ss.at[g, q], l_rs.at[g, q], tdev(q))
+
+    def low_products(g):
+        for k in range(max(1, 4 * g), 4 * g + 4):
+            r_copy((-ORDER[k]) % NZ).wait_recv()
+        low_all = lax.dot_general(
+            db[...].reshape(8 * 48, PART), rrecv[TOK * g : TOK * (g + 1), :],
+            (((1,), (1,)), ((), ())), preferred_element_type=F32,
+        )
+        mine = jnp.zeros((48, TOK), F32)
+        for a in range(8):
+            mine = mine + jnp.where(
+                a8_row[g][0:1, :] == float(a), low_all[48 * a : 48 * a + 48, :], 0.0
+            )
+        low_mine[g] = mine
+        low_s[g] = mine.astype(BF)
+        for q in range(1, NT):
+            go(l_copy(g, q))
+
+    which = ((lax.broadcasted_iota(jnp.int32, (TOK, 384), 1) >> 4) & 7).astype(F32)
+
+    def low_table(g):
+        total = low_mine[g]
+        for q in range(1, NT):
+            l_copy(g, q).wait_recv()
+            total = total + low_r[g, q].astype(F32)
+        total = total.astype(BF)
+        wide = jnp.concatenate(
+            [total[0:16]] * 8 + [total[16:32]] * 8 + [total[32:48]] * 8, axis=0
+        )
+        for k in range(4 * g, 4 * g + 4):
+            got = lax.dot_general(
+                place[k], wide, (((1,), (1,)), ((), ())), preferred_element_type=F32
+            )
+            low_l[k] = jnp.where(which == a8_of[k][:, 0:1], got, 0.0).astype(BF)
 
     def product(c, i):
         a = act[pl.ds(2 * i, 2)].reshape(2 * TOK, PART)
         w = wkvb[...] if c == 0 else wqb[:, CW * (c - 1) : CW * c]
         return jnp.dot(a, w, preferred_element_type=F32).reshape(2, TOK, CW)
 
-    def base(c):
+    def base(c, g):
         def tile(i, carry):
             part[c, pl.ds(2 * i, 2)] = product(c, i)
             return carry
 
-        lax.fori_loop(0, NZ // 2, tile, 0)
-
+        lax.fori_loop(2 * g, 2 * g + 2, tile, 0)
+
+    for copy in own:
+        copy.wait()
+    y_wait(0)
+    low_products(1)
+    y_pump(5)
+    for g in range(3):
+        for k in range(4):
+            p_copy(g, k).wait_recv()
+    y_wait(1)
+    y_wait(2)
+    base(0, 1)
+    low_products(0)
+    base(0, 0)
+    low_table(1)
     y_wait(3)
     y_wait(4)
-    base(0)
-    y_pump(5)
-
-    y_wait(0)
-    for q in ORDER[1:]:
-        r_copy(q).wait_recv()
-    low_all = lax.dot_general(
-        db[...].reshape(8 * 48, PART), rrecv[...], (((1,), (1,)), ((), ())),
-        preferred_element_type=F32,
-    )
-    low_mine = jnp.zeros((48, NZ * ROWS), F32)
-    for a in range(8):
-        low_mine = low_mine + jnp.where(
-            a8_row[0:1, :] == float(a), low_all[48 * a : 48 * a + 48, :], 0.0
-        )
-    low_s[...] = low_mine.astype(BF)
-
-    def l_copy(q):
-        return remote(low_s, low_r.at[q], l_ss.at[q], l_rs.at[q], tdev(q))
-
-    for q in range(1, NT):
-        go(l_copy(q))
-    y_wait(5)
-    base(1)
-    y_pump(6)
-    for q in range(1, NT):
-        l_copy(q).wait_recv()
-    low_sum = low_mine
-    for q in range(1, NT):
-        low_sum = low_sum + low_r[q].astype(F32)
-    low_sum = low_sum.astype(BF)
-    wide = jnp.concatenate(
-        [low_sum[0:16]] * 8 + [low_sum[16:32]] * 8 + [low_sum[32:48]] * 8, axis=0
-    )
-    which = ((lax.broadcasted_iota(jnp.int32, (TOK, 384), 1) >> 4) & 7).astype(F32)
-    for k in range(NZ):
-        got = lax.dot_general(
-            place[k], wide, (((1,), (1,)), ((), ())), preferred_element_type=F32
-        )
-        low_l[k] = jnp.where(which == a8_of[k][:, 0:1], got, 0.0).astype(BF)
-
-    y_wait(1)
-    y_wait(2)
 
     def z_copy(c, way, h):
         k = POS[h if way == 0 else NZ - h]
@@ -416,13 +416,13 @@
             d = jnp.dot(ll[:, 0:128], u_q, preferred_element_type=F32)
         return (0.5 * d.astype(BF).astype(F32)).reshape(2, TOK, CW)
 
-    def complete(c):
+    def complete(c, g):
         def tile(i, carry):
-            here = part[c, pl.ds(2 * i, 2)] if c < 2 else product(c, i)
+            here = product(c, i) if c > 0 else part[c, pl.ds(2 * i, 2)]
             part[c, pl.ds(2 * i, 2)] = here + change(c, i)
             return carry
 
-        lax.fori_loop(0, NZ // 2, tile, 0)
+        lax.fori_loop(2 * g, 2 * g + 2, tile, 0)
 
     def ring(c, h):
         for way in range(2):
@@ -436,23 +436,40 @@
             sendb[c, k] = total.astype(BF)
             go(z_copy(c, way, h))
 
-    for c in range(2):
-        complete(c)
-        ring(c, 4)
+    complete(0, 1)
+    ring(0, 4)
+    y_pump(6)
+    low_table(0)
     y_pump(7)
+    y_wait(5)
+    complete(1, 1)
+    ring(1, 4)
+    complete(0, 0)
     ring(0, 3)
+    y_pump(8)
+    complete(1, 0)
     ring(1, 3)
     for c in range(2, CHUNKS):
         y_wait(4 + c)
-        complete(c)
+        complete(c, 1)
         ring(c, 4)
-        if c == 2:
-            y_pump(8)
     for c in range(2, CHUNKS):
         ring(c, 3)
-    for h in (2, 1):
-        for c in range(CHUNKS):
-            ring(c, h)
+        complete(c, 0)
+    for c in range(CHUNKS):
+        ring(c, 2)
+    pos_m = jnp.broadcast_to(pos_c, (TOK, TOK))
+    cos = jnp.zeros((TOK, TOK), F32)
+    sin = jnp.zeros((TOK, TOK), F32)
+    for p in range(8):
+        here = pos_m == float(p)
+        cos = jnp.where(here, rope[p : p + 1, :], cos)
+        sin = jnp.where(here, rope[8 + p : 9 + p, :], sin)
+    cosb[...] = cos
+    sinb[...] = sin
+
+    for c in range(CHUNKS):
+        ring(c, 1)
 
     def final(c):
         z_copy(c, 0, 1).wait_recv()
@@ -520,9 +537,13 @@
             jax.ShapeDtypeStruct((TOK, HEAD), BF),
             jax.ShapeDtypeStruct((TOK, HEAD), BF),
         ),
-        in_specs=[any_spec, vmem, vmem, vmem, vmem] + [any_spec] * 6,
+        in_specs=[any_spec] * 11,
         out_specs=(vmem, vmem, vmem),
         scratch_shapes=[
+            pltpu.VMEM((WIDTH // 128, 128), BF),
+            pltpu.VMEM((1, TOK), jnp.int32),
+            pltpu.VMEM((1, count), jnp.int32),
+            pltpu.VMEM((16, 128), F32),
             pltpu.VMEM((TOK, WIDTH), BF),
             pltpu.VMEM((16, WIDTH), BF),
             pltpu.VMEM((WIDTH // 128, 128), F32),
@@ -538,10 +559,10 @@
             pltpu.VMEM((8, 48, PART), BF),
             pltpu.VMEM((8, 16, PART), BF),
             pltpu.VMEM((8, 32, HEAD), BF),
-            pltpu.VMEM((NZ, TOK, NZ * ROWS), BF),
+            pltpu.VMEM((NZ, TOK, TOK), BF),
             pltpu.VMEM((NZ, TOK, 128), F32),
-            pltpu.VMEM((48, NZ * ROWS), BF),
-            pltpu.VMEM((NT, 48, NZ * ROWS), BF),
+            pltpu.VMEM((2, 48, TOK), BF),
+            pltpu.VMEM((2, NT, 48, TOK), BF),
             pltpu.VMEM((NZ, TOK, 384), BF),
             pltpu.VMEM((CHUNKS, NZ, TOK, CW), F32),
             pltpu.VMEM((CHUNKS, NZ, TOK, CW), BF),
@@ -549,14 +570,14 @@
             pltpu.VMEM((TOK, TOK), F32),
             pltpu.VMEM((TOK, TOK), F32),
             pltpu.VMEM((TOK, TOK), F32),
-            dma((11,)),
+            dma((15,)),
             dma((9, 4)), dma((9, 4)),
             dma((NZ,)), dma((NZ,)),
             dma((NZ,)), dma((NZ,)),
             dma((NZ,)), dma((NZ,)),
             dma((3, 4)), dma((3, 4)),
             dma((3, 4)), dma((3, 4)),
-            dma((NT,)), dma((NT,)),
+            dma((2, NT)), dma((2, NT)),
             dma((CHUNKS, 2, 4)), dma((CHUNKS, 2, 4)),
         ],
         compiler_params=pltpu.CompilerParams(

time: 77.3 us -> 70.8 us (0.916)
  Pallas kernels: 76.5 us -> 69.5 us
    pallas_call x1, Pallas kernels: 74.8 us -> 67.8 us  [per_device(): call(hidden, gain.reshape(WIDTH // 128, 128), adapter.reshape(1, TOK), st...]
where the time goes in v4:
time: 70.8 us; the launch traced here: 70.1 us
  Pallas kernels  69.5 us (98%)
    pallas_call x1, Pallas kernels, per_device(): call(hidden, gain.reshape(WIDTH // 128, 128), adapter.reshape(1, TOK), st...  67.8 us
    pallas_call x1, Pallas kernels, per_device(): pl.pallas_call(forward, out_shape=tuple((jax.ShapeDtypeStruct(o.shape, o....  1.7 us

profile of v4, /device:TPU:6, one launch (start us, length us, event | category | flops | bytes accessed | tf_op | source)
XLA Modules:
  0.0 70.1 jit_solution(16635511824137812700)
XLA Ops:
  0.6 67.8 %shard_map.130 = (bf16[128,1024]{1,0:T(8,128)(2,1)}, bf16[128,128]{1,0:T(8,128)(2,1)}, bf16[128,128]{1,0:T(8,128)(2,1)}) custom-call(bf16[128,8192]{1,0:T(8,128)(2,1)} %hid.1, bf16[64,128]{1,0:T(8,128)(2,1)} %bitcast.3, s32[1,128]{1,0:T(1,128)} %bitcast.4, s32[1,64]{1,0:T(1,128)} %bitcast.5, f32[16,128]{1,0:T(8,128)} %constant.2.clone.rope_h, ...), custom_call_target="tpu_custom_call" | custom-call | tf_op jit(solution)/shard_map/pallas_call | solution.py:587
  68.4 1.7 %shard_map.131 = (bf16[128,1024]{1,0:T(8,128)(2,1)}, bf16[128,128]{1,0:T(8,128)(2,1)}, bf16[128,128]{1,0:T(8,128)(2,1)}) custom-call(bf16[128,1024]{1,0:T(8,128)(2,1)} %get-tuple-element.6.a, bf16[128,128]{1,0:T(8,128)(2,1)} %get-tuple-element.7.b, bf16[128,128]{1,0:T(8,128)(2,1)} %get-tuple-element.8.c), custom_call_target="tpu_custom_call" | custom-call | tf_op jit(solution)/shard_map/pallas_call | solution.py:595

commit v5 on v4

--- a/solution.py
+++ b/solution.py
@@ -144,16 +144,6 @@
     hid_copy = pltpu.make_async_copy(hid, hidv, loc_sem.at[0])
     hid_copy.start()
 
-    pl.semaphore_wait(barrier, 7 + 7 + 2)
-    for i in range(AHEAD):
-        y_start(i)
-    own = []
-    for i in range(len(items)):
-        src, region, _ = items[i]
-        copy = pltpu.make_async_copy(src, region(y), loc_sem.at[1 + i])
-        copy.start()
-        own.append(copy)
-
     def inverse_root(ref, rows):
         total = jnp.zeros((16, 128), F32)
         for k in range(8):
@@ -174,6 +164,16 @@
         asend[m // 8, :, d : d + 128] = (
             hid16[:, c].astype(F32) * s16 * gainf[m : m + 1, :]
         ).astype(BF)
+
+    pl.semaphore_wait(barrier, 7 + 7 + 2)
+    for i in range(AHEAD):
+        y_start(i)
+    own = []
+    for i in range(len(items)):
+        src, region, _ = items[i]
+        copy = pltpu.make_async_copy(src, region(y), loc_sem.at[1 + i])
+        copy.start()
+        own.append(copy)
 
     def a_copy(q):
         k = POS[(-q) % NZ]
@@ -299,10 +299,8 @@
     x_send(1)
     y_pump(1)
     x_send(0)
+    y_pump(2)
     x_forward(2)
-    y_pump(2)
-    x_forward(1)
-    x_last(2)
 
     for q in ORDER[1:]:
         m_copy(q).wait_recv()
@@ -318,10 +316,12 @@
         a8 = ((code.astype(jnp.int32) >> 5) & 7).astype(F32).astype(BF)
         a8_row[k // 4] = a8_row[k // 4] + jnp.dot(a8, hot, preferred_element_type=F32)
 
+    x_forward(1)
     y_pump(3)
     x_forward(0)
+    y_pump(4)
+    x_last(2)
     x_last(1)
-    y_pump(4)
     x_last(0)
 
     low_mine = [None, None]
@@ -375,19 +375,23 @@
 
         lax.fori_loop(2 * g, 2 * g + 2, tile, 0)
 
+    def p_wait(g):
+        for k in range(4):
+            p_copy(g, k).wait_recv()
+
     for copy in own:
         copy.wait()
     y_wait(0)
     low_products(1)
     y_pump(5)
-    for g in range(3):
-        for k in range(4):
-            p_copy(g, k).wait_recv()
+    p_wait(2)
+    p_wait(1)
     y_wait(1)
     y_wait(2)
     base(0, 1)
+    p_wait(0)
+    base(0, 0)
     low_products(0)
-    base(0, 0)
     low_table(1)
     y_wait(3)
     y_wait(4)

time: 70.8 us -> 70.5 us (level)
  no operation moved by 1% of the time
where the time goes in v5:
time: 70.5 us; the launch traced here: 70.4 us
  Pallas kernels  69.7 us (99%)
    pallas_call x1, Pallas kernels, per_device(): call(hidden, gain.reshape(WIDTH // 128, 128), adapter.reshape(1, TOK), st...  68 us
    pallas_call x1, Pallas kernels, per_device(): pl.pallas_call(forward, out_shape=tuple((jax.ShapeDtypeStruct(o.shape, o....  1.7 us

profile of v5, /device:TPU:6, one launch (start us, length us, event | category | flops | bytes accessed | tf_op | source)
XLA Modules:
  0.0 70.4 jit_solution(11412919148860293417)
XLA Ops:
  0.6 68.0 %shard_map.130 = (bf16[128,1024]{1,0:T(8,128)(2,1)}, bf16[128,128]{1,0:T(8,128)(2,1)}, bf16[128,128]{1,0:T(8,128)(2,1)}) custom-call(bf16[128,8192]{1,0:T(8,128)(2,1)} %hid.1, bf16[64,128]{1,0:T(8,128)(2,1)} %bitcast.3, s32[1,128]{1,0:T(1,128)} %bitcast.4, s32[1,64]{1,0:T(1,128)} %bitcast.5, f32[16,128]{1,0:T(8,128)} %constant.2.clone.rope_h, ...), custom_call_target="tpu_custom_call" | custom-call | tf_op jit(solution)/shard_map/pallas_call | solution.py:591
  68.7 1.7 %shard_map.131 = (bf16[128,1024]{1,0:T(8,128)(2,1)}, bf16[128,128]{1,0:T(8,128)(2,1)}, bf16[128,128]{1,0:T(8,128)(2,1)}) custom-call(bf16[128,1024]{1,0:T(8,128)(2,1)} %get-tuple-element.6.a, bf16[128,128]{1,0:T(8,128)(2,1)} %get-tuple-element.7.b, bf16[128,128]{1,0:T(8,128)(2,1)} %get-tuple-element.8.c), custom_call_target="tpu_custom_call" | custom-call | tf_op jit(solution)/shard_map/pallas_call | solution.py:599
